TPU v7x, 128 devices: a whole 4x4x4 slice. The times are simulated.
128 devices in a mesh: section: 8 (over y_lo, x), fsdp: 16 (over y_hi, z, core).
Axes of the slice: x: 4, y: 4 (y_hi: 2, y_lo: 2; y = y_hi * 2 + y_lo), z: 4, core: 2. Of those that a mesh axis runs over, the one named last changes fastest.
Arguments:
- section_input: bfloat16 [8, 4096, 4096], P('section', 'fsdp'), may hold values from -6 to 6
- segment_ids: int32 [8, 4096], P('section', 'fsdp'), may hold values from 0 to 2, never falling along the last dimension, each value on 1 to 3072 neighbouring positions
- query_weight: bfloat16 [8, 4096, 2048], P('section', 'fsdp'), as said below
- keyval_weight: bfloat16 [8, 4096, 512], P('section', 'fsdp'), as said below
- out_weight: bfloat16 [8, 2048, 4096], P('section', None, 'fsdp'), may hold values from -0.125 to 0.125
Outputs:
- passed: bfloat16 [8, 4096, 4096], P('section', 'fsdp')
Inputs may be any that keep to these rules, and one draw needn't show every extreme that they name: `query_weight`: query projection weights. `keyval_weight`: key and value projection weights.
All inputs are finite; a program needn't handle non-finite values.
Results may differ from a plain program's by a relative error of at most 0.012.
The roundings to bfloat16 on the way count: a program that leaves them out, or rounds other values in their place, can miss the bound.
Values may be sent and summed in bfloat16 or wider, within the bound.
A program may use at most 192 MiB of HBM per device.

v0:
```python
import math

import jax
import jax.numpy as jnp
from jax import lax
from jax.sharding import PartitionSpec as P

QUERY_HEADS = 32
KEY_HEADS = 4
HEAD_SIZE = 64
LOOKBACK_SPAN = 2048


def from_behind(value, axis, steps):
    count = lax.axis_size(axis)
    pairs = [(source, (source + steps) % count) for source in range(count)]
    return lax.ppermute(value, axis, pairs)


def normed(values):
    widened = values.astype(jnp.float32)
    scaled = widened * lax.rsqrt(jnp.mean(widened * widened, axis=-1, keepdims=True) + 1e-05)
    return scaled.astype(jnp.bfloat16)


def body(section_input, segment_ids, query_weight, keyval_weight, out_weight):
    hidden = section_input[0]
    segments = segment_ids[0]
    resident_rows = hidden.shape[0]
    queries_per_group = QUERY_HEADS // KEY_HEADS
    device_pos = lax.axis_index("fsdp")
    normal_rows = normed(hidden)
    fresh_query = jnp.dot(
        normal_rows,
        lax.all_gather(query_weight, "fsdp", axis=1, tiled=True)[0],
        preferred_element_type=jnp.float32,
    )
    keyval_new = jnp.dot(
        normal_rows,
        lax.all_gather(keyval_weight, "fsdp", axis=1, tiled=True)[0],
        preferred_element_type=jnp.float32,
    )
    query_rows = fresh_query.astype(jnp.bfloat16).reshape(
        resident_rows, KEY_HEADS, queries_per_group, HEAD_SIZE
    )
    key_value_rows = keyval_new.astype(jnp.bfloat16)
    query_pos = device_pos * resident_rows + jnp.arange(resident_rows, dtype=jnp.int32)
    start_state = (
        jnp.full((KEY_HEADS, queries_per_group, resident_rows), -1e30, jnp.float32),
        jnp.zeros((KEY_HEADS, queries_per_group, resident_rows), jnp.float32),
        jnp.zeros((KEY_HEADS, queries_per_group, resident_rows, HEAD_SIZE), jnp.float32),
    )
    key_value_pairs = lax.all_gather(key_value_rows, "fsdp", axis=0, tiled=True)
    key_segs = lax.all_gather(segments, "fsdp", axis=0, tiled=True)
    piece_rows = key_value_pairs.shape[0]
    rows_per_block = math.gcd(piece_rows, 512)
    total_blocks = piece_rows // rows_per_block
    key_tiles = key_value_pairs.reshape(total_blocks, rows_per_block, 2 * KEY_HEADS * HEAD_SIZE)
    seg_blocks = key_segs.reshape(total_blocks, rows_per_block)

    def one_block(inner, items):
        peak_now, sum_now, acc_now = inner
        value_tiles, block_segs, block_index = items
        key_lines = value_tiles[:, : KEY_HEADS * HEAD_SIZE].reshape(
            rows_per_block, KEY_HEADS, HEAD_SIZE
        )
        value_lines = value_tiles[:, KEY_HEADS * HEAD_SIZE :].reshape(
            rows_per_block, KEY_HEADS, HEAD_SIZE
        )
        key_pos = block_index * rows_per_block + jnp.arange(rows_per_block, dtype=jnp.int32)
        scores = jnp.einsum(
            "qhgd,khd->hgqk", query_rows, key_lines, preferred_element_type=jnp.float32
        ) * HEAD_SIZE ** (-0.5)
        visible = (segments[:, None] == block_segs[None, :]) & (
            key_pos[None, :] <= query_pos[:, None]
        )
        visible = (
            visible
            & (key_pos[None, :] > query_pos[:, None] - LOOKBACK_SPAN)
            & (key_pos[None, :] >= 0)
        )
        scores = jnp.where(visible, scores, -1e30)
        peak_new = jnp.maximum(peak_now, jnp.max(scores, axis=-1))
        weights = jnp.where(visible, jnp.exp(scores - peak_new[..., None]), 0.0)
        factor = jnp.exp(peak_now - peak_new)
        sum_new = sum_now * factor + jnp.sum(weights, axis=-1)
        mixed_part = jnp.einsum(
            "hgqk,khd->hgqd",
            weights.astype(jnp.bfloat16),
            value_lines,
            preferred_element_type=jnp.float32,
        )
        acc_new = acc_now * factor[..., None] + mixed_part
        return ((peak_new, sum_new, acc_new), None)

    final_state, unused = lax.scan(
        one_block, start_state, (key_tiles, seg_blocks, jnp.arange(total_blocks, dtype=jnp.int32))
    )
    row_peak, weight_sum, accum = final_state
    mixed_heads = accum / weight_sum[..., None]
    attended = (
        jnp.transpose(mixed_heads, (2, 0, 1, 3))
        .reshape(resident_rows, QUERY_HEADS * HEAD_SIZE)
        .astype(jnp.bfloat16)
    )
    projected = jnp.dot(
        attended,
        lax.all_gather(out_weight, "fsdp", axis=2, tiled=True)[0],
        preferred_element_type=jnp.float32,
    )
    updated = (hidden.astype(jnp.float32) + projected).astype(jnp.bfloat16)
    passed = from_behind(updated, "section", 1)
    return passed[None]


def solution(mesh):
    return jax.shard_map(
        body,
        mesh=mesh,
        in_specs=(
            P("section", "fsdp", None),
            P("section", "fsdp"),
            P("section", "fsdp", None),
            P("section", "fsdp", None),
            P("section", None, "fsdp"),
        ),
        out_specs=P("section", "fsdp", None),
        check_vma=False,
    )
```

profile of v0, /device:TPU:1, one launch (start us, length us, event | category | flops | bytes accessed | tf_op | source)
XLA Modules:
  0.0 521.7 jit_solution(2219916994663872434)
XLA Ops:
  8.1 2.1 fusion.26
  10.2 58.8 %all-gather.6.cloned.1.call-done = bf16[1,4096,512]{2,1,0:T(8,128)(2,1)} async-done(((bf16[1,256,512]{2,1,0:T(8,128)(2,1)}), bf16[1,4096,512]{2,1,0:T(8,128)(2,1)}) %all-gather.6.cloned.1.call-update) | async-done | bytes 4194320 | tf_op jit(solution)/shard_map/all_gather | solution.py:40
  68.9 4.8 fusion.34
  74.4 20.1 %all-gather = s32[1,4096]{1,0:T(1,128)S(1)} all-gather(s32[1,256]{1,0:T(1,128)S(1)} %copy-done.3), channel_id=2, replica_groups=mesh['section'=8,'fsdp'=16] {'fsdp'}, dimensions={1}, use_global_device_ids=true | all-gather | bytes 17408 | tf_op jit(solution)/shard_map/all_gather | solution.py:54
  95.8 82.8 %all-gather.10.cloned.1.call-done = bf16[1,4096,2048]{2,1,0:T(8,128)(2,1)} async-done(((bf16[1,256,2048]{2,1,0:T(8,128)(2,1)}), bf16[1,4096,2048]{2,1,0:T(8,128)(2,1)}) %all-gather.10.cloned.1.call-update) | async-done | bytes 16777232 | tf_op jit(solution)/shard_map/all_gather | solution.py:35
  178.6 8.3 %fusion.30 = bf16[256,2048]{1,0:T(8,128)(2,1)S(1)} fusion(bf16[1,4096,2048]{2,1,0:T(8,128)(2,1)} %all-gather.10.cloned.1.call-done, bf16[1,256,4096]{2,1,0:T(8,128)(2,1)S(1)} %copy-done.1, f32[256]{0:T(256)S(1)} %add_rsqrt_fusion), kind=kOutput, calls=%fused_computation.37 | convolution fusion | flops 4298637312 | bytes 19923968 | tf_op jit(solution)/shard_map/dot_general | solution.py:33
  187.5 46.6 %all-gather.8.cloned.1.call-done = bf16[4096,512]{1,0:T(8,128)(2,1)} async-done(((bf16[256,512]{1,0:T(8,128)(2,1)}), bf16[4096,512]{1,0:T(8,128)(2,1)}) %all-gather.8.cloned.1.call-update) | async-done | bytes 4194320 | tf_op jit(solution)/shard_map/all_gather | solution.py:53
  234.1 218.1 %while.17 = (s32[]{:T(128)}, f32[4,8,256]{2,1,0:T(8,128)S(1)}, f32[4,8,256]{2,1,0:T(8,128)S(1)}, f32[4,8,256,64]{2,3,1,0:T(8,128)}, s32[1,256]{1,0:T(1,128)S(1)}...) while((s32[]{:T(128)}, f32[4,8,256]{2,1,0:T(8,128)S(1)}, ...), condition=%wide.region_4.5_spmd.clone, body=%wide.region_1.4_spmd.clone.sunk | while | flops 1130670080 | bytes 127418568 | solution.py:96
  237.1 7.4 %fusion.58 = (f32[4,8,256]{2,1,0:T(8,128)S(1)}, f32[4,512,256,8]{2,1,3,0:T(8,128)}) fusion(pred[256,512]{0,1:T(8,128)(4,1)S(1)} %and_and_fusion.2, bf16[512,4,64,1]{0,2,3,1:T(8,128)(2,1)S(1)} %bitcast.94, bf16[256,4,8,64]{0,3,2,1:T(8,128)(2,1)S(1)} %get-tuple-element.328), kind=kOutput, calls=%fused_computation.3.clone.1 | convolution fusion | flops 549445632 | bytes 18251776 | tf_op jit(solution)/shard_map/while/body/eval_jaxpr/qhgd,khd->hgqk/dot_general | solution.py:71
  244.6 8.6 %fusion.59 = f32[4,8,256]{2,1,0:T(8,128)S(1)} fusion(f32[4,512,256,8]{2,1,3,0:T(8,128)} %get-tuple-element.290, f32[4,8,256]{2,1,0:T(8,128)S(1)} %select_maximum_fusion.2, pred[256,512]{0,1:T(8,128)(4,1)S(1)} %and_and_fusion.2), kind=kLoop, calls=%fused_computation.5.clone.1 | loop fusion | flops 20963328 | bytes 16973824 | tf_op jit(solution)/shard_map/while/body/eval_jaxpr/reduce_sum | solution.py:86
  253.2 2.4 copy-done
  255.6 5.1 fusion.61
  262.4 1.1 constant_dynamic-slice_fusion.5
  263.7 7.2 %fusion.58 = (f32[4,8,256]{2,1,0:T(8,128)S(1)}, f32[4,512,256,8]{2,1,3,0:T(8,128)}) fusion(pred[256,512]{0,1:T(8,128)(4,1)S(1)} %and_and_fusion.2, bf16[512,4,64,1]{0,2,3,1:T(8,128)(2,1)S(1)} %bitcast.94, bf16[256,4,8,64]{0,3,2,1:T(8,128)(2,1)S(1)} %get-tuple-element.328), kind=kOutput, calls=%fused_computation.3.clone.1 | convolution fusion | flops 549445632 | bytes 18251776 | tf_op jit(solution)/shard_map/while/body/eval_jaxpr/qhgd,khd->hgqk/dot_general | solution.py:71
  270.9 8.4 %fusion.59 = f32[4,8,256]{2,1,0:T(8,128)S(1)} fusion(f32[4,512,256,8]{2,1,3,0:T(8,128)} %get-tuple-element.290, f32[4,8,256]{2,1,0:T(8,128)S(1)} %select_maximum_fusion.2, pred[256,512]{0,1:T(8,128)(4,1)S(1)} %and_and_fusion.2), kind=kLoop, calls=%fused_computation.5.clone.1 | loop fusion | flops 20963328 | bytes 16973824 | tf_op jit(solution)/shard_map/while/body/eval_jaxpr/reduce_sum | solution.py:86
  279.4 2.3 copy-done
  281.7 6.3 %fusion.61 = f32[4,8,256,64]{2,3,1,0:T(8,128)} fusion(f32[4,8,256,64]{2,3,1,0:T(8,128)} %get-tuple-element.310, bf16[512,4,64,1]{0,2,3,1:T(8,128)(2,1)S(1)} %bitcast.95, f32[4,512,256,8]{2,1,3,0:T(8,128)S(1)} %copy-done, f32[4,8,256]{2,1,0:T(8,128)S(1)} %select_maximum_fusion.2, pred[256,512]{0,1:T(8,128)(4,1)S(1)} %and_and_fusion.2, ...), kind=kOutput, calls=%fused_computation.9.clone.1 | convolution fusion | flops 559415296 | bytes 21430272 | tf_op jit(solution)/shard_map/while/body/eval_jaxpr/hgqk,khd->hgqd/dot_general | solution.py:87
  289.7 1.1 constant_dynamic-slice_fusion.5
  291.0 7.1 %fusion.58 = (f32[4,8,256]{2,1,0:T(8,128)S(1)}, f32[4,512,256,8]{2,1,3,0:T(8,128)}) fusion(pred[256,512]{0,1:T(8,128)(4,1)S(1)} %and_and_fusion.2, bf16[512,4,64,1]{0,2,3,1:T(8,128)(2,1)S(1)} %bitcast.94, bf16[256,4,8,64]{0,3,2,1:T(8,128)(2,1)S(1)} %get-tuple-element.328), kind=kOutput, calls=%fused_computation.3.clone.1 | convolution fusion | flops 549445632 | bytes 18251776 | tf_op jit(solution)/shard_map/while/body/eval_jaxpr/qhgd,khd->hgqk/dot_general | solution.py:71
  298.2 8.8 %fusion.59 = f32[4,8,256]{2,1,0:T(8,128)S(1)} fusion(f32[4,512,256,8]{2,1,3,0:T(8,128)} %get-tuple-element.290, f32[4,8,256]{2,1,0:T(8,128)S(1)} %select_maximum_fusion.2, pred[256,512]{0,1:T(8,128)(4,1)S(1)} %and_and_fusion.2), kind=kLoop, calls=%fused_computation.5.clone.1 | loop fusion | flops 20963328 | bytes 16973824 | tf_op jit(solution)/shard_map/while/body/eval_jaxpr/reduce_sum | solution.py:86
  307.0 2.4 copy-done
  309.4 6.3 %fusion.61 = f32[4,8,256,64]{2,3,1,0:T(8,128)} fusion(f32[4,8,256,64]{2,3,1,0:T(8,128)} %get-tuple-element.310, bf16[512,4,64,1]{0,2,3,1:T(8,128)(2,1)S(1)} %bitcast.95, f32[4,512,256,8]{2,1,3,0:T(8,128)S(1)} %copy-done, f32[4,8,256]{2,1,0:T(8,128)S(1)} %select_maximum_fusion.2, pred[256,512]{0,1:T(8,128)(4,1)S(1)} %and_and_fusion.2, ...), kind=kOutput, calls=%fused_computation.9.clone.1 | convolution fusion | flops 559415296 | bytes 21430272 | tf_op jit(solution)/shard_map/while/body/eval_jaxpr/hgqk,khd->hgqd/dot_general | solution.py:87
  318.8 7.1 %fusion.58 = (f32[4,8,256]{2,1,0:T(8,128)S(1)}, f32[4,512,256,8]{2,1,3,0:T(8,128)}) fusion(pred[256,512]{0,1:T(8,128)(4,1)S(1)} %and_and_fusion.2, bf16[512,4,64,1]{0,2,3,1:T(8,128)(2,1)S(1)} %bitcast.94, bf16[256,4,8,64]{0,3,2,1:T(8,128)(2,1)S(1)} %get-tuple-element.328), kind=kOutput, calls=%fused_computation.3.clone.1 | convolution fusion | flops 549445632 | bytes 18251776 | tf_op jit(solution)/shard_map/while/body/eval_jaxpr/qhgd,khd->hgqk/dot_general | solution.py:71
  325.9 8.3 %fusion.59 = f32[4,8,256]{2,1,0:T(8,128)S(1)} fusion(f32[4,512,256,8]{2,1,3,0:T(8,128)} %get-tuple-element.290, f32[4,8,256]{2,1,0:T(8,128)S(1)} %select_maximum_fusion.2, pred[256,512]{0,1:T(8,128)(4,1)S(1)} %and_and_fusion.2), kind=kLoop, calls=%fused_computation.5.clone.1 | loop fusion | flops 20963328 | bytes 16973824 | tf_op jit(solution)/shard_map/while/body/eval_jaxpr/reduce_sum | solution.py:86
  334.3 2.9 copy-done
  337.2 6.3 %fusion.61 = f32[4,8,256,64]{2,3,1,0:T(8,128)} fusion(f32[4,8,256,64]{2,3,1,0:T(8,128)} %get-tuple-element.310, bf16[512,4,64,1]{0,2,3,1:T(8,128)(2,1)S(1)} %bitcast.95, f32[4,512,256,8]{2,1,3,0:T(8,128)S(1)} %copy-done, f32[4,8,256]{2,1,0:T(8,128)S(1)} %select_maximum_fusion.2, pred[256,512]{0,1:T(8,128)(4,1)S(1)} %and_and_fusion.2, ...), kind=kOutput, calls=%fused_computation.9.clone.1 | convolution fusion | flops 559415296 | bytes 21430272 | tf_op jit(solution)/shard_map/while/body/eval_jaxpr/hgqk,khd->hgqd/dot_general | solution.py:87
  345.2 1.1 constant_dynamic-slice_fusion.5
  346.6 7.1 %fusion.58 = (f32[4,8,256]{2,1,0:T(8,128)S(1)}, f32[4,512,256,8]{2,1,3,0:T(8,128)}) fusion(pred[256,512]{0,1:T(8,128)(4,1)S(1)} %and_and_fusion.2, bf16[512,4,64,1]{0,2,3,1:T(8,128)(2,1)S(1)} %bitcast.94, bf16[256,4,8,64]{0,3,2,1:T(8,128)(2,1)S(1)} %get-tuple-element.328), kind=kOutput, calls=%fused_computation.3.clone.1 | convolution fusion | flops 549445632 | bytes 18251776 | tf_op jit(solution)/shard_map/while/body/eval_jaxpr/qhgd,khd->hgqk/dot_general | solution.py:71
  353.7 8.3 %fusion.59 = f32[4,8,256]{2,1,0:T(8,128)S(1)} fusion(f32[4,512,256,8]{2,1,3,0:T(8,128)} %get-tuple-element.290, f32[4,8,256]{2,1,0:T(8,128)S(1)} %select_maximum_fusion.2, pred[256,512]{0,1:T(8,128)(4,1)S(1)} %and_and_fusion.2), kind=kLoop, calls=%fused_computation.5.clone.1 | loop fusion | flops 20963328 | bytes 16973824 | tf_op jit(solution)/shard_map/while/body/eval_jaxpr/reduce_sum | solution.py:86
  362.1 2.3 copy-done
  364.4 6.3 %fusion.61 = f32[4,8,256,64]{2,3,1,0:T(8,128)} fusion(f32[4,8,256,64]{2,3,1,0:T(8,128)} %get-tuple-element.310, bf16[512,4,64,1]{0,2,3,1:T(8,128)(2,1)S(1)} %bitcast.95, f32[4,512,256,8]{2,1,3,0:T(8,128)S(1)} %copy-done, f32[4,8,256]{2,1,0:T(8,128)S(1)} %select_maximum_fusion.2, pred[256,512]{0,1:T(8,128)(4,1)S(1)} %and_and_fusion.2, ...), kind=kOutput, calls=%fused_computation.9.clone.1 | convolution fusion | flops 559415296 | bytes 21430272 | tf_op jit(solution)/shard_map/while/body/eval_jaxpr/hgqk,khd->hgqd/dot_general | solution.py:87
  373.8 7.1 %fusion.58 = (f32[4,8,256]{2,1,0:T(8,128)S(1)}, f32[4,512,256,8]{2,1,3,0:T(8,128)}) fusion(pred[256,512]{0,1:T(8,128)(4,1)S(1)} %and_and_fusion.2, bf16[512,4,64,1]{0,2,3,1:T(8,128)(2,1)S(1)} %bitcast.94, bf16[256,4,8,64]{0,3,2,1:T(8,128)(2,1)S(1)} %get-tuple-element.328), kind=kOutput, calls=%fused_computation.3.clone.1 | convolution fusion | flops 549445632 | bytes 18251776 | tf_op jit(solution)/shard_map/while/body/eval_jaxpr/qhgd,khd->hgqk/dot_general | solution.py:71
  380.9 8.3 %fusion.59 = f32[4,8,256]{2,1,0:T(8,128)S(1)} fusion(f32[4,512,256,8]{2,1,3,0:T(8,128)} %get-tuple-element.290, f32[4,8,256]{2,1,0:T(8,128)S(1)} %select_maximum_fusion.2, pred[256,512]{0,1:T(8,128)(4,1)S(1)} %and_and_fusion.2), kind=kLoop, calls=%fused_computation.5.clone.1 | loop fusion | flops 20963328 | bytes 16973824 | tf_op jit(solution)/shard_map/while/body/eval_jaxpr/reduce_sum | solution.py:86
  389.2 2.3 copy-done
  391.5 6.3 %fusion.61 = f32[4,8,256,64]{2,3,1,0:T(8,128)} fusion(f32[4,8,256,64]{2,3,1,0:T(8,128)} %get-tuple-element.310, bf16[512,4,64,1]{0,2,3,1:T(8,128)(2,1)S(1)} %bitcast.95, f32[4,512,256,8]{2,1,3,0:T(8,128)S(1)} %copy-done, f32[4,8,256]{2,1,0:T(8,128)S(1)} %select_maximum_fusion.2, pred[256,512]{0,1:T(8,128)(4,1)S(1)} %and_and_fusion.2, ...), kind=kOutput, calls=%fused_computation.9.clone.1 | convolution fusion | flops 559415296 | bytes 21430272 | tf_op jit(solution)/shard_map/while/body/eval_jaxpr/hgqk,khd->hgqd/dot_general | solution.py:87
  400.9 7.1 %fusion.58 = (f32[4,8,256]{2,1,0:T(8,128)S(1)}, f32[4,512,256,8]{2,1,3,0:T(8,128)}) fusion(pred[256,512]{0,1:T(8,128)(4,1)S(1)} %and_and_fusion.2, bf16[512,4,64,1]{0,2,3,1:T(8,128)(2,1)S(1)} %bitcast.94, bf16[256,4,8,64]{0,3,2,1:T(8,128)(2,1)S(1)} %get-tuple-element.328), kind=kOutput, calls=%fused_computation.3.clone.1 | convolution fusion | flops 549445632 | bytes 18251776 | tf_op jit(solution)/shard_map/while/body/eval_jaxpr/qhgd,khd->hgqk/dot_general | solution.py:71
  408.0 8.3 %fusion.59 = f32[4,8,256]{2,1,0:T(8,128)S(1)} fusion(f32[4,512,256,8]{2,1,3,0:T(8,128)} %get-tuple-element.290, f32[4,8,256]{2,1,0:T(8,128)S(1)} %select_maximum_fusion.2, pred[256,512]{0,1:T(8,128)(4,1)S(1)} %and_and_fusion.2), kind=kLoop, calls=%fused_computation.5.clone.1 | loop fusion | flops 20963328 | bytes 16973824 | tf_op jit(solution)/shard_map/while/body/eval_jaxpr/reduce_sum | solution.py:86
  416.4 2.3 copy-done
  418.7 6.3 %fusion.61 = f32[4,8,256,64]{2,3,1,0:T(8,128)} fusion(f32[4,8,256,64]{2,3,1,0:T(8,128)} %get-tuple-element.310, bf16[512,4,64,1]{0,2,3,1:T(8,128)(2,1)S(1)} %bitcast.95, f32[4,512,256,8]{2,1,3,0:T(8,128)S(1)} %copy-done, f32[4,8,256]{2,1,0:T(8,128)S(1)} %select_maximum_fusion.2, pred[256,512]{0,1:T(8,128)(4,1)S(1)} %and_and_fusion.2, ...), kind=kOutput, calls=%fused_computation.9.clone.1 | convolution fusion | flops 559415296 | bytes 21430272 | tf_op jit(solution)/shard_map/while/body/eval_jaxpr/hgqk,khd->hgqd/dot_general | solution.py:87
  428.1 7.1 %fusion.58 = (f32[4,8,256]{2,1,0:T(8,128)S(1)}, f32[4,512,256,8]{2,1,3,0:T(8,128)}) fusion(pred[256,512]{0,1:T(8,128)(4,1)S(1)} %and_and_fusion.2, bf16[512,4,64,1]{0,2,3,1:T(8,128)(2,1)S(1)} %bitcast.94, bf16[256,4,8,64]{0,3,2,1:T(8,128)(2,1)S(1)} %get-tuple-element.328), kind=kOutput, calls=%fused_computation.3.clone.1 | convolution fusion | flops 549445632 | bytes 18251776 | tf_op jit(solution)/shard_map/while/body/eval_jaxpr/qhgd,khd->hgqk/dot_general | solution.py:71
  435.2 8.3 %fusion.59 = f32[4,8,256]{2,1,0:T(8,128)S(1)} fusion(f32[4,512,256,8]{2,1,3,0:T(8,128)} %get-tuple-element.290, f32[4,8,256]{2,1,0:T(8,128)S(1)} %select_maximum_fusion.2, pred[256,512]{0,1:T(8,128)(4,1)S(1)} %and_and_fusion.2), kind=kLoop, calls=%fused_computation.5.clone.1 | loop fusion | flops 20963328 | bytes 16973824 | tf_op jit(solution)/shard_map/while/body/eval_jaxpr/reduce_sum | solution.py:86
  443.6 2.3 copy-done
  445.9 6.3 %fusion.61 = f32[4,8,256,64]{2,3,1,0:T(8,128)} fusion(f32[4,8,256,64]{2,3,1,0:T(8,128)} %get-tuple-element.310, bf16[512,4,64,1]{0,2,3,1:T(8,128)(2,1)S(1)} %bitcast.95, f32[4,512,256,8]{2,1,3,0:T(8,128)S(1)} %copy-done, f32[4,8,256]{2,1,0:T(8,128)S(1)} %select_maximum_fusion.2, pred[256,512]{0,1:T(8,128)(4,1)S(1)} %and_and_fusion.2, ...), kind=kOutput, calls=%fused_computation.9.clone.1 | convolution fusion | flops 559415296 | bytes 21430272 | tf_op jit(solution)/shard_map/while/body/eval_jaxpr/hgqk,khd->hgqd/dot_general | solution.py:87
  452.2 2.0 divide_convert_fusion
  454.4 10.5 %fusion.23 = bf16[256,4096]{1,0:T(8,128)(2,1)S(1)} fusion(bf16[256,2048]{0,1:T(8,128)(2,1)S(1)} %bitcast.96, bf16[1,2048,4096]{2,1,0:T(8,128)(2,1)} %all-gather.12.cloned.1.call-done, bf16[1,256,4096]{2,1,0:T(8,128)(2,1)S(1)} %copy-done.2), kind=kOutput, calls=%fused_computation.32 | convolution fusion | flops 4298113024 | bytes 22020096 | tf_op jit(solution)/shard_map/dot_general | solution.py:106
  465.0 1.3 collective-permute-start
  466.2 47.7 %collective-permute-done = bf16[256,4096]{1,0:T(8,128)(2,1)S(1)} collective-permute-done((bf16[256,4096]{1,0:T(8,128)(2,1)S(1)}, bf16[256,4096]{1,0:T(8,128)(2,1)S(1)}, u32[]{:S(2)}, u32[]{:S(2)}) %collective-permute-start) | collective-permute-done | bytes 2097184 | tf_op jit(solution)/shard_map/ppermute | solution.py:17
  513.9 1.3 copy.31
  (125 shorter events, 19.4 us)
Async XLA Ops:
  6.5 62.4 %all-gather.6.cloned.1.call-start = ((), (), s32[]{:S(2)}) async-start(), calls=%async_computation | async-start | bytes 4456448 | tf_op jit(solution)/shard_map/all_gather | solution.py:40
  7.3 171.3 %all-gather.10.cloned.1.call-start = ((), (), s32[]{:S(2)}) async-start(), calls=%async_computation.2 | async-start | bytes 17825792 | tf_op jit(solution)/shard_map/all_gather | solution.py:35
  8.0 226.1 %all-gather.8.cloned.1.call-start = ((), (), s32[]{:S(2)}) async-start(), calls=%async_computation.1 | async-start | bytes 4456448 | tf_op jit(solution)/shard_map/all_gather | solution.py:53
  10.1 64.2 %copy-start.3 = (s32[1,256]{1,0:T(1,128)S(1)}, s32[1,256]{1,0:T(1,128)}, u32[]{:S(2)}) copy-start(s32[1,256]{1,0:T(1,128)} %param.8) | copy-start | bytes 3076
  10.2 168.4 %copy-start.1 = (bf16[1,256,4096]{2,1,0:T(8,128)(2,1)S(1)}, bf16[1,256,4096]{2,1,0:T(8,128)(2,1)}, u32[]{:S(2)}) copy-start(bf16[1,256,4096]{2,1,0:T(8,128)(2,1)} %param.7) | copy-start | bytes 6291460
  73.8 380.4 %all-gather.12.cloned.1.call-start = ((), (), s32[]{:S(2)}) async-start(), calls=%async_computation.3 | async-start | bytes 17825792 | tf_op jit(solution)/shard_map/all_gather | solution.py:108
  244.6 11.0 %copy-start = (f32[4,512,256,8]{2,1,3,0:T(8,128)S(1)}, f32[4,512,256,8]{2,1,3,0:T(8,128)}, u32[]{:S(2)}) copy-start(f32[4,512,256,8]{2,1,3,0:T(8,128)} %get-tuple-element.290) | copy-start | bytes 50331652 | tf_op jit(solution)/shard_map/while
  270.9 10.7 %copy-start = (f32[4,512,256,8]{2,1,3,0:T(8,128)S(1)}, f32[4,512,256,8]{2,1,3,0:T(8,128)}, u32[]{:S(2)}) copy-start(f32[4,512,256,8]{2,1,3,0:T(8,128)} %get-tuple-element.290) | copy-start | bytes 50331652 | tf_op jit(solution)/shard_map/while
  298.2 11.3 %copy-start = (f32[4,512,256,8]{2,1,3,0:T(8,128)S(1)}, f32[4,512,256,8]{2,1,3,0:T(8,128)}, u32[]{:S(2)}) copy-start(f32[4,512,256,8]{2,1,3,0:T(8,128)} %get-tuple-element.290) | copy-start | bytes 50331652 | tf_op jit(solution)/shard_map/while
  325.9 11.3 %copy-start = (f32[4,512,256,8]{2,1,3,0:T(8,128)S(1)}, f32[4,512,256,8]{2,1,3,0:T(8,128)}, u32[]{:S(2)}) copy-start(f32[4,512,256,8]{2,1,3,0:T(8,128)} %get-tuple-element.290) | copy-start | bytes 50331652 | tf_op jit(solution)/shard_map/while
  353.7 10.7 %copy-start = (f32[4,512,256,8]{2,1,3,0:T(8,128)S(1)}, f32[4,512,256,8]{2,1,3,0:T(8,128)}, u32[]{:S(2)}) copy-start(f32[4,512,256,8]{2,1,3,0:T(8,128)} %get-tuple-element.290) | copy-start | bytes 50331652 | tf_op jit(solution)/shard_map/while
  380.9 10.7 %copy-start = (f32[4,512,256,8]{2,1,3,0:T(8,128)S(1)}, f32[4,512,256,8]{2,1,3,0:T(8,128)}, u32[]{:S(2)}) copy-start(f32[4,512,256,8]{2,1,3,0:T(8,128)} %get-tuple-element.290) | copy-start | bytes 50331652 | tf_op jit(solution)/shard_map/while
  408.0 10.7 %copy-start = (f32[4,512,256,8]{2,1,3,0:T(8,128)S(1)}, f32[4,512,256,8]{2,1,3,0:T(8,128)}, u32[]{:S(2)}) copy-start(f32[4,512,256,8]{2,1,3,0:T(8,128)} %get-tuple-element.290) | copy-start | bytes 50331652 | tf_op jit(solution)/shard_map/while
  435.2 10.7 %copy-start = (f32[4,512,256,8]{2,1,3,0:T(8,128)S(1)}, f32[4,512,256,8]{2,1,3,0:T(8,128)}, u32[]{:S(2)}) copy-start(f32[4,512,256,8]{2,1,3,0:T(8,128)} %get-tuple-element.290) | copy-start | bytes 50331652 | tf_op jit(solution)/shard_map/while
  452.2 2.2 copy-start.2
  465.0 48.9 %collective-permute-start = (bf16[256,4096]{1,0:T(8,128)(2,1)S(1)}, bf16[256,4096]{1,0:T(8,128)(2,1)S(1)}, u32[]{:S(2)}, u32[]{:S(2)}) collective-permute-start(bf16[256,4096]{1,0:T(8,128)(2,1)S(1)} %fusion.23), channel_id=1, source_target_pairs={{0,16},{16,32},{32,48},{48,64},{64,80},{80,96},{96,112},{112,0},{1... | collective-permute-start | bytes 6291464 | tf_op jit(solution)/shard_map/ppermute | solution.py:17
Sparse Core Ops, SparseCore 0:
  9.8 59.0 all-gather.5
  71.4 107.1 all-gather.9
  181.1 52.9 all-gather.7
  236.2 116.7 all-gather.11
where the time goes:
time: 523 us; the launch traced here: 522 us
  waiting for transfers between devices  238 us (46%)
  matrix products  130 us (25%)
  other arithmetic  74.8 us (14%)
  local copies, waits for them, and re-layouts  37.9 us (7%)
  blocking collectives  20.1 us (4%)
  between operations  13.2 us (3%)
  loops' own time  6.13 us (1%)
    all_gather x1, waiting for transfers between devices, body(): lax.all_gather(query_weight, 'fsdp', axis=1, tiled=True)[0]  82.8 us
    reduce_sum x8, other arithmetic, one_block(): sum_new = sum_now * factor + jnp.sum(weights, axis=-1)  67.5 us
    all_gather x1, waiting for transfers between devices, body(): lax.all_gather(keyval_weight, 'fsdp', axis=1, tiled=True)[0]  58.8 us
    dot_general x8, matrix products, one_block(): jnp.einsum('qhgd,khd->hgqk', query_rows, key_lines, preferred_element_typ...  57.2 us
    dot_general x8, matrix products, one_block(): jnp.einsum('hgqk,khd->hgqd', weights.astype(jnp.bfloat16), value_lines, p...  49.4 us
    ppermute x1, waiting for transfers between devices, from_behind(): return lax.ppermute(value, axis, pairs)  47.7 us
    all_gather x1, waiting for transfers between devices, body(): key_value_pairs = lax.all_gather(key_value_rows, 'fsdp', axis=0, tiled=True)  46.6 us
    all_gather x1, blocking collectives, body(): key_segs = lax.all_gather(segments, 'fsdp', axis=0, tiled=True)  20.1 us
  transfers between devices with their start and end apart: 5, of which 4 were waited for; matrix products, arithmetic and copies ran while one was open for 41% of the time, Pallas kernels for 0%

commit v1 on v0

v1 whole, which is shorter than its diff:
```python
import jax
import jax.numpy as jnp
from jax import lax
from jax.experimental import pallas as pl
from jax.experimental.pallas import tpu as pltpu
from jax.sharding import Mesh, PartitionSpec as P

BF = jnp.bfloat16
F32 = jnp.float32
MESH = pl.DeviceIdType.MESH

KV, Q0, Q1, Q2, Q3, KX, O0, O1 = range(8)


def kernel(hid, segrow, segcol, wq, wkv, wo, out,
           x, wb, wob, kvb, qs, att, hf, outb, sbuf, acc, qst, sgr, sgc, lod,
           ss, rs, ls, ns, nr, ws, wr, hs, hr, hl, gs, gr, xs, xr, a_s, a_r, ps, pr):
    sec, yh, z, c = (lax.axis_index(n) for n in ("section", "yh", "z", "core"))
    oc = 1 - c
    b = yh * 4 + z
    zp, zm, zz = (z + 1) % 4, (z + 3) % 4, (z + 2) % 4
    oy = 1 - yh
    SIB = (sec, yh, z, oc)
    YP = (sec, oy, z, c)
    ZP = (sec, yh, zp, c)
    ZM = (sec, yh, zm, c)
    nxt, prv = (sec + 1) % 8, (sec + 7) % 8
    NX = [(nxt, yh, z, 0), (nxt, yh, z, 1)]
    PV = [(prv, yh, z, 0), (prv, yh, z, 1)]

    def rcopy(src, dst, send, recv, dev):
        return pltpu.make_async_remote_copy(
            src_ref=src, dst_ref=dst, send_sem=send, recv_sem=recv,
            device_id=dev, device_id_type=MESH)

    bar = pltpu.get_barrier_semaphore()
    for d in [SIB, YP, ZP, ZM] + NX + PV:
        pl.semaphore_signal(bar, inc=1, device_id=d, device_id_type=MESH)
    pl.semaphore_wait(bar, 8)

    def rows256(k):
        return pl.ds(pl.multiple_of(256 * k, 256), 256)

    def blk(ci, owner):
        if ci <= Q3:
            return wb.at[ci, owner]
        if ci == KX:
            return kvb.at[owner]
        return wob.at[ci - O0, owner]

    def half(ci, owner, h):
        n = 256 if ci <= Q3 else (272 if ci == KX else 1024)
        return blk(ci, owner).at[pl.ds(n * h, n)]

    OWN, PAR = b, oy * 4 + z
    own = lambda dy, dz: ((yh + dy) % 2) * 4 + (z + dz) % 4

    def sendc(ci, i):
        src, dev = {
            0: lambda: (blk(ci, OWN), YP),
            1: lambda: (blk(ci, OWN), ZP),
            2: lambda: (blk(ci, OWN), ZM),
            3: lambda: (blk(ci, PAR), ZP),
            4: lambda: (blk(ci, PAR), ZM),
            5: lambda: (half(ci, own(0, 3), 0), ZP),
            6: lambda: (half(ci, own(0, 1), 1), ZM),
            7: lambda: (blk(ci, own(0, 2)), YP),
        }[i]()
        return rcopy(src, src, ss.at[ci, i], rs.at[ci, i], dev)

    def waitc(ci, i):
        dst = {
            0: lambda: blk(ci, PAR),
            1: lambda: blk(ci, own(0, 3)),
            2: lambda: blk(ci, own(0, 1)),
            3: lambda: blk(ci, own(1, 3)),
            4: lambda: blk(ci, own(1, 1)),
            5: lambda: half(ci, own(0, 2), 0),
            6: lambda: half(ci, own(0, 2), 1),
            7: lambda: blk(ci, own(1, 2)),
        }[i]()
        rcopy(dst, dst, ss.at[ci, i], rs.at[ci, i], YP).wait_recv()

    def own_pieces(ci):
        if ci == KV:
            return [(wkv, 128 * c, 128 * oc, 0, 128), (wkv, 256 + 128 * c, 256 + 128 * oc, 128, 128)]
        k = ci - Q0
        return [(wq, 1024 * c + 256 * k, 1024 * oc + 256 * k, 0, 256)]

    def fill_copies(ci):
        loc, rem = [], []
        for n, (w, mine, theirs, lane, width) in enumerate(own_pieces(ci)):
            dst = wb.at[ci, b, rows256(c), pl.ds(lane, width)]
            loc.append(pltpu.make_async_copy(
                w.at[:, pl.ds(pl.multiple_of(mine, 128), width)], dst, ls.at[ci, n]))
            rem.append(rcopy(
                w.at[:, pl.ds(pl.multiple_of(theirs, 128), width)], dst,
                ws.at[ci, n], wr.at[ci, n], SIB))
        return loc, rem

    def fill_waits(ci):
        for n, (w, mine, theirs, lane, width) in enumerate(own_pieces(ci)):
            dst = wb.at[ci, b, rows256(c), pl.ds(lane, width)]
            pltpu.make_async_copy(
                w.at[:, pl.ds(pl.multiple_of(mine, 128), width)], dst, ls.at[ci, n]).wait()
        for n, (w, mine, theirs, lane, width) in enumerate(own_pieces(ci)):
            dst = wb.at[ci, b, rows256(oc), pl.ds(lane, width)]
            rcopy(dst, dst, ws.at[ci, n], wr.at[ci, n], SIB).wait_recv()

    def wo_fill(h):
        return pltpu.make_async_copy(wo.at[:, pl.ds(128 * h, 128)], wob.at[h, b], ls.at[O0 + h, 0])

    for ci in (KV, Q0, Q1, Q2, Q3):
        loc, rem = fill_copies(ci)
        for d in rem + loc:
            d.start()
    for h in (0, 1):
        wo_fill(h).start()

    g1 = rcopy(sgr.at[c], sgr.at[c], gs.at[0], gr.at[0], SIB)
    g2 = rcopy(sgc.at[c], sgc.at[c], gs.at[1], gr.at[1], SIB)
    sgr[c] = segrow[...]
    sgc[c] = segcol[...]
    g1.start()
    g2.start()

    def hid_cols(o, cc):
        return hid.at[:, pl.ds(pl.multiple_of(256 * (2 * o + cc), 256), 256)]

    def hid_remote(o):
        return rcopy(hid_cols(o, oc), hf.at[c, o], hs.at[o], hr.at[o], SIB)

    def hid_local(o):
        return pltpu.make_async_copy(hid_cols(o, c), hf.at[c, o], hl.at[o])

    def phase_a(ci):
        if ci <= Q3:
            fill_waits(ci)
        elif ci >= O0:
            wo_fill(ci - O0).wait()
        for i in (0, 1, 2):
            sendc(ci, i).start()

    def phase_b(ci):
        waitc(ci, 0)
        sendc(ci, 3).start()
        sendc(ci, 4).start()
        waitc(ci, 1)
        sendc(ci, 5).start()
        waitc(ci, 2)
        sendc(ci, 6).start()

    def phase_c(ci):
        waitc(ci, 5)
        waitc(ci, 6)
        sendc(ci, 7).start()
        waitc(ci, 3)
        waitc(ci, 4)

    def phase_d(ci):
        waitc(ci, 7)

    def gemm(ci):
        acc[...] = jnp.zeros_like(acc)

        def step(o, carry):
            acc[...] += jnp.dot(x[o], wb[ci, o], preferred_element_type=F32)
            return carry

        lax.fori_loop(0, 8, step, 0)

    phase_a(KV)
    phase_a(Q0)

    def norm(i, carry):
        r = pl.ds(pl.multiple_of(32 * i, 32), 32)
        v = hid[r, :].astype(F32)
        v = v * lax.rsqrt(jnp.mean(v * v, axis=-1, keepdims=True) + 1e-05)
        v = v.astype(BF)
        dst = pl.ds(pl.multiple_of(256 * c + 32 * i, 32), 32)
        for o in range(8):
            x[o, dst, :] = v[:, 512 * o:512 * o + 512]
        return carry

    lax.fori_loop(0, 8, norm, 0)
    xc = rcopy(x.at[:, rows256(c)], x.at[:, rows256(c)], ns, nr, SIB)
    xc.start()
    for o in range(8):
        hid_remote(o).start()
        hid_local(o).start()

    phase_b(KV)
    phase_a(Q1)
    phase_c(KV)
    phase_b(Q0)
    xw = x.at[:, rows256(oc)]
    rcopy(xw, xw, ns, nr, SIB).wait_recv()
    phase_d(KV)
    gemm(KV)
    kvb[b, 0:512, :] = acc[...].astype(BF)
    for i in (0, 1):
        w_ = (sgr.at[oc], sgc.at[oc])[i]
        rcopy(w_, w_, gs.at[i], gr.at[i], SIB).wait_recv()
    kvb[b, 512:528, :] = sgr[0]
    kvb[b, 528:544, :] = sgr[1]
    phase_a(KX)

    def put_q(k):
        gemm(Q0 + k)
        qs[2 * k] = acc[:, 0:128].astype(BF)
        qs[2 * k + 1] = acc[:, 128:256].astype(BF)

    phase_c(Q0)
    phase_b(KX)
    phase_a(Q2)
    phase_b(Q1)
    phase_d(Q0)
    put_q(0)
    phase_c(KX)
    phase_c(Q1)
    phase_a(Q3)
    phase_b(Q2)
    phase_d(KX)

    lane = lax.broadcasted_iota(jnp.int32, (256, 128), 1)
    row = lax.broadcasted_iota(jnp.int32, (256, 128), 0)
    below1 = jnp.zeros((16, 256), F32)
    below2 = jnp.zeros((16, 256), F32)
    for o in range(8):
        for t in (512, 528):
            g = kvb[o, t:t + 16, :].astype(F32)
            below1 = below1 + jnp.where(g < 0.5, 1.0, 0.0)
            below2 = below2 + jnp.where(g < 1.5, 1.0, 0.0)
    n1 = jnp.sum(below1[0:8], axis=-1, keepdims=True)[0:1, :]
    n2 = jnp.sum(below2[0:8], axis=-1, keepdims=True)[0:1, :]
    for j in (0, 1):
        g = sgc[j].astype(F32)
        start = jnp.where(g < 0.5, 0.0, jnp.where(g < 1.5, n1, n2)).astype(jnp.int32)
        pos = 512 * b + 256 * j + row
        lod[j] = jnp.maximum(start, pos - 2047) - lane

    low = lane < 64

    def attend(k):
        first_head = k < 2

        def one(it, carry):
            p = 2 * k + it // 2
            j = it % 2
            jr = rows256(j)
            q2 = qs[p, jr, :].astype(F32)
            qr = pltpu.roll(q2, 64, 1)
            zero = jnp.zeros_like(q2)
            if first_head:
                qe, qo = jnp.where(low, q2, zero), jnp.where(low, qr, zero)
            else:
                qe, qo = jnp.where(low, zero, qr), jnp.where(low, zero, q2)
            qst[0:256, :] = qe.astype(BF)
            qst[256:512, :] = qo.astype(BF)
            d1 = lod[j]
            m = jnp.full((512, 128), -1e30, F32)
            for t in range(9):
                kb = (2 * b + j + t + 8) % 16
                kk = kvb[kb // 2, rows256(kb % 2), 0:128]
                s = lax.dot_general(qst[...], kk, (((1,), (1,)), ((), ())),
                                    preferred_element_type=F32)
                base = 256 * (2 * b + j + t) - 2048
                for u in (0, 1):
                    ok = d1 <= base + 128 * u
                    if t == 8:
                        ok = ok & (row - lane >= 128 * u)
                    ok = jnp.concatenate([ok, ok], axis=0)
                    su = jnp.where(ok, s[:, 128 * u:128 * u + 128], -1e30)
                    sbuf[t, :, 128 * u:128 * u + 128] = su
                    m = jnp.maximum(m, su)
            mm = jnp.max(m, axis=-1, keepdims=True)
            l = jnp.zeros((512, 128), F32)
            o_ = jnp.zeros((512, 128), F32)
            for t in range(9):
                kb = (2 * b + j + t + 8) % 16
                vv = kvb[kb // 2, rows256(kb % 2), 128:256]
                w = jnp.exp((sbuf[t] - mm) * 0.125)
                l = l + w[:, 0:128] + w[:, 128:256]
                o_ = o_ + jnp.dot(w.astype(BF), vv, preferred_element_type=F32)
            o_ = o_ / jnp.sum(l, axis=-1, keepdims=True)
            oe, oo = o_[0:256], o_[256:512]
            if first_head:
                res = jnp.where(low, oe, pltpu.roll(oo, 64, 1))
            else:
                res = jnp.where(low, pltpu.roll(oe, 64, 1), oo)
            att[jr, pl.ds(pl.multiple_of(1024 * c + 128 * p, 128), 128)] = res.astype(BF)
            return carry

        lax.fori_loop(0, 4, one, 0)
        cols = pl.ds(pl.multiple_of(1024 * c + 256 * k, 256), 256)
        rcopy(att.at[:, cols], att.at[:, cols], a_s.at[k], a_r.at[k], SIB).start()

    attend(0)
    phase_d(Q1)
    put_q(1)
    phase_a(O0)
    phase_c(Q2)
    phase_b(Q3)
    attend(1)
    phase_d(Q2)
    put_q(2)
    phase_a(O1)
    phase_c(Q3)
    phase_b(O0)
    attend(2)
    phase_d(Q3)
    put_q(3)
    phase_c(O0)
    phase_b(O1)
    attend(3)

    for k in range(4):
        cols = pl.ds(pl.multiple_of(1024 * oc + 256 * k, 256), 256)
        w_ = att.at[:, cols]
        rcopy(w_, w_, a_s.at[k], a_r.at[k], SIB).wait_recv()
    for o in range(8):
        hid_local(o).wait()
        w_ = hf.at[oc, o]
        rcopy(w_, w_, hs.at[o], hr.at[o], SIB).wait_recv()

    def out_cols(o, cc, h):
        return out.at[:, pl.ds(pl.multiple_of(256 * (2 * o + cc) + 128 * h, 128), 128)]

    def pass_copy(h, o, cc):
        return rcopy(outb.at[h, o, cc], out_cols(o, c, h), ps.at[h, o, cc], pr.at[h, o, c], NX[cc])

    def project(h, n, dy, dz):
        def step(i, carry):
            o = own(dy(i), dz(i))
            v = jnp.dot(att[...], wob[h, o], preferred_element_type=F32)
            for cc in (0, 1):
                r = v[256 * cc:256 * cc + 256] + hf[cc, o, :, 128 * h:128 * h + 128].astype(F32)
                outb[h, o, cc] = r.astype(BF)
                pass_copy(h, o, cc).start()
            return carry

        lax.fori_loop(0, n, step, 0)

    def project_b(h):
        project(h, 2, lambda i: i, lambda i: 0)
        project(h, 2, lambda i: 0, lambda i: 1 + 2 * i)

    def project_c(h):
        project(h, 2, lambda i: 1, lambda i: 1 + 2 * i)
        project(h, 1, lambda i: 0, lambda i: 2)

    def project_d(h):
        project(h, 1, lambda i: 1, lambda i: 2)

    project_b(0)
    project_c(0)
    phase_d(O0)
    project_d(0)
    project_b(1)
    phase_c(O1)
    project_c(1)
    phase_d(O1)
    project_d(1)

    for ci in range(8):
        for i in range(8):
            sendc(ci, i).wait_send()
    for ci in (KV, Q0, Q1, Q2, Q3):
        for d in fill_copies(ci)[1]:
            d.wait_send()
    g1.wait_send()
    g2.wait_send()
    xc.wait_send()
    for o in range(8):
        hid_remote(o).wait_send()
    for k in range(4):
        cols = pl.ds(pl.multiple_of(1024 * c + 256 * k, 256), 256)
        rcopy(att.at[:, cols], att.at[:, cols], a_s.at[k], a_r.at[k], SIB).wait_send()
    for h in (0, 1):
        for o in range(8):
            for cc in (0, 1):
                pass_copy(h, o, cc).wait_send()
                w_ = out_cols(o, cc, h)
                rcopy(w_, w_, ps.at[h, o, cc], pr.at[h, o, cc], NX[cc]).wait_recv()


def body(section_input, segment_ids, query_weight, keyval_weight, out_weight):
    hidden = section_input[0]
    seg = segment_ids[0].astype(BF)
    segrow = jnp.broadcast_to(seg[None, :], (16, 256))
    segcol = jnp.broadcast_to(seg[:, None], (256, 128))
    vm = pl.BlockSpec(memory_space=pltpu.VMEM)
    hb = pl.BlockSpec(memory_space=pl.ANY)
    dma = pltpu.SemaphoreType.DMA
    res = pl.pallas_call(
        kernel,
        out_shape=jax.ShapeDtypeStruct((256, 4096), BF),
        in_specs=[vm, vm, vm, hb, hb, hb],
        out_specs=hb,
        scratch_shapes=[
            pltpu.VMEM((8, 512, 512), BF),
            pltpu.VMEM((5, 8, 512, 256), BF),
            pltpu.VMEM((2, 8, 2048, 128), BF),
            pltpu.VMEM((8, 544, 256), BF),
            pltpu.VMEM((8, 512, 128), BF),
            pltpu.VMEM((512, 2048), BF),
            pltpu.VMEM((2, 8, 256, 256), BF),
            pltpu.VMEM((2, 8, 2, 256, 128), BF),
            pltpu.VMEM((9, 512, 256), F32),
            pltpu.VMEM((512, 256), F32),
            pltpu.VMEM((512, 128), BF),
            pltpu.VMEM((2, 16, 256), BF),
            pltpu.VMEM((2, 256, 128), BF),
            pltpu.VMEM((2, 256, 128), jnp.int32),
            dma((8, 8)), dma((8, 8)),
            dma((8, 2)),
            dma, dma,
            dma((5, 2)), dma((5, 2)),
            dma((8,)), dma((8,)), dma((8,)),
            dma((2,)), dma((2,)),
            dma, dma,
            dma((4,)), dma((4,)),
            dma((2, 8, 2)), dma((2, 8, 2)),
        ],
        compiler_params=pltpu.CompilerParams(
            collective_id=0, has_side_effects=True, vmem_limit_bytes=58 << 20),
        name="layer",
    )(hidden, segrow, segcol, query_weight[0], keyval_weight[0], out_weight[0])
    return res[None]


def solution(mesh):
    fine = Mesh(mesh.devices.reshape(8, 2, 4, 2), ("section", "yh", "z", "core"))
    tok = ("yh", "z", "core")
    return jax.shard_map(
        body,
        mesh=fine,
        in_specs=(
            P("section", tok, None),
            P("section", tok),
            P("section", tok, None),
            P("section", tok, None),
            P("section", None, tok),
        ),
        out_specs=P("section", tok, None),
        check_vma=False,
    )
```

time: 523 us -> 228 us (0.44)
  waiting for transfers between devices: 238 us -> 0 us
  Pallas kernels: 0 us -> 222 us
  matrix products: 130 us -> 0 us
  other arithmetic: 74.8 us -> 0.7 us
  local copies, waits for them, and re-layouts: 37.9 us -> 4.46 us
  blocking collectives: 20.1 us -> 0 us
  between operations: 13.2 us -> 0.01 us
  loops' own time: 6.13 us -> 0 us
    pallas_call x0 -> x1, Pallas kernels: none -> 222 us  [body(): pl.pallas_call(kernel, out_shape=jax.ShapeDtypeStruct((256, 4096), BF), i...]
    all_gather x4 -> x0, waiting for transfers between devices: 188 us -> none  [the longest x1 82.8 us: body(): lax.all_gather(query_weight, 'fsdp', axis=1, tiled=True)[0]]
    dot_general x19 -> x0, matrix products: 130 us -> none  [the longest x8 57.2 us: one_block(): jnp.einsum('qhgd,khd->hgqk', query_rows, key_lines, preferred_element_typ...]
    reduce_sum x9 -> x0, other arithmetic: 69.6 us -> none  [the longest x8 67.5 us: one_block(): sum_new = sum_now * factor + jnp.sum(weights, axis=-1)]
    ppermute x1 -> x0, waiting for transfers between devices: 47.7 us -> none  [from_behind(): return lax.ppermute(value, axis, pairs)]
    all_gather x1 -> x0, blocking collectives: 20.1 us -> none  [body(): key_segs = lax.all_gather(segments, 'fsdp', axis=0, tiled=True)]
    while x24 -> x0, local copies, waits for them, and re-layouts: 19.3 us -> none
    dynamic_slice x32 -> x0, local copies, waits for them, and re-layouts: 15.7 us -> none  [body(): lax.scan(one_block, start_state, (key_tiles, seg_blocks, jnp.arange(total...]
  transfers between devices with their start and end apart: 5 -> 0, of which waited for: 4 -> 0; matrix products, arithmetic and copies ran while one was open for 41% -> 0% of each run, Pallas kernels for 0% -> 0%
where the time goes in v1:
time: 228 us; the launch traced here: 227 us
  Pallas kernels  222 us (97%)
  local copies, waits for them, and re-layouts  4.46 us (2%)
    pallas_call x1, Pallas kernels, body(): pl.pallas_call(kernel, out_shape=jax.ShapeDtypeStruct((256, 4096), BF), i...  222 us

profile of v1, /device:TPU:1, one launch (start us, length us, event | category | flops | bytes accessed | tf_op | source)
XLA Modules:
  0.0 226.7 jit_solution(6665221086188528065)
XLA Ops:
  0.0 0.7 convert_reduce_fusion
  0.7 0.6 broadcast_in_dim.18.segrow
  1.3 0.7 broadcast_in_dim.19.segcol
  2.0 221.6 %layer.1 = bf16[256,4096]{1,0:T(8,128)(2,1)} custom-call(bf16[256,4096]{1,0:T(8,128)(2,1)} %bitcast.6, bf16[16,256]{1,0:T(8,128)(2,1)} %broadcast_in_dim.18.segrow, bf16[256,128]{1,0:T(8,128)(2,1)} %broadcast_in_dim.19.segcol, bf16[256,2048]{1,0:T(8,128)(2,1)} %bitcast.7, bf16[256,512]{1,0:T(8,128)(2,1)} %bitcast.9, bf16[2048,256]{1,0:T(8,128)(2,1)} %bitcast.8), custom_call_target="tpu_custom_call" | custom-call | tf_op jit(solution)/shard_map/layer/pallas_call | solution.py:395
  223.6 3.1 %copy.7 = bf16[1,256,4096]{2,1,0:T(8,128)(2,1)} copy(bf16[1,256,4096]{2,1,0:T(8,128)(2,1)} %bitcast.5) | data formatting | bytes 4194304

commit v2 on v0

v2 whole, which is shorter than its diff:
```python
import jax
import jax.numpy as jnp
from jax import lax
from jax.experimental import pallas as pl
from jax.experimental.pallas import tpu as pltpu
from jax.sharding import Mesh, PartitionSpec as P

BF = jnp.bfloat16
F32 = jnp.float32
MESH = pl.DeviceIdType.MESH
EXP_SCALE = 0.125 * 1.4426950408889634

KV, QA, QB, KX = range(4)


def kernel(hid, seg, wq, wkv, wo, out,
           x, wqb, wkvb, wob, kvb, qs, att, atx, hf, outb, accq, acck, ostat, sgr, lod,
           fs, fr, fl, zs, zr, os_, or_, ol, xs, xr, hs, hr, hl, gs, gr, axs, axr, ps, pr, rly, rs, rr):
    sec, yh, z, c = (lax.axis_index(n) for n in ("section", "yh", "z", "core"))
    oc, oy = 1 - c, 1 - yh
    u = 2 * yh + c
    u_sib, u_y, u_yx = 2 * yh + oc, 2 * oy + c, 2 * oy + oc
    b = yh * 4 + z
    zp, zm = (z + 1) % 4, (z + 3) % 4
    SIB = (sec, yh, z, oc)
    YP = (sec, oy, z, c)
    YX = (sec, oy, z, oc)
    ZP = (sec, yh, zp, c)
    ZM = (sec, yh, zm, c)
    nxt, prv = (sec + 1) % 8, (sec + 7) % 8
    NX = [(nxt, yh, z, 0), (nxt, yh, z, 1)]
    PV = [(prv, yh, z, 0), (prv, yh, z, 1)]
    wrap = sec % 4 == 3
    MID = ((sec + 4) % 8, yh, z, c)
    FAR = [((sec + 5) % 8, yh, z, k) for k in (0, 1)]
    NEAR = [((sec + 3) % 8, yh, z, k) for k in (0, 1)]

    def rcopy(src, dst, send, recv, dev):
        return pltpu.make_async_remote_copy(
            src_ref=src, dst_ref=dst, send_sem=send, recv_sem=recv,
            device_id=dev, device_id_type=MESH)

    def got(dst, send, recv):
        rcopy(dst, dst, send, recv, SIB).wait_recv()

    def al(v, n):
        return pl.multiple_of(v, n)

    def r256(k):
        return pl.ds(al(256 * k, 256), 256)

    bar = pltpu.get_barrier_semaphore()
    for d in [SIB, YP, YX, ZP, ZM, MID] + NX + PV + FAR + NEAR:
        pl.semaphore_signal(bar, inc=1, device_id=d, device_id_type=MESH)
    pl.semaphore_wait(bar, 14)

    def quarter(ci, v):
        if ci == KV:
            return wkv.at[:, pl.ds(al(128 * v, 128), 128)]
        return wq.at[:, pl.ds(al(512 * v + 256 * (ci - QA), 256), 256)]

    def rb(ci, zo):
        if ci == KV:
            return wkvb.at[zo]
        if ci == KX:
            return kvb.at[zo]
        return wqb.at[ci - QA, zo]

    def fill(ci, n):
        v, dev = [(u_y, YP), (u_yx, YX), (u_sib, SIB)][n]
        return rcopy(quarter(ci, v), rb(ci, z).at[r256(u)], fs.at[ci, n], fr.at[ci, u], dev)

    def fill_local(ci):
        return pltpu.make_async_copy(quarter(ci, u), rb(ci, z).at[r256(u)], fl.at[ci])

    def fill_wait(ci):
        fill_local(ci).wait()
        for v in (u_sib, u_y, u_yx):
            got(rb(ci, z).at[r256(v)], fs.at[ci, 0], fr.at[ci, v])

    def rhalf(ci, zo, h):
        n = 576 if ci == KX else 512
        return rb(ci, zo).at[pl.ds(n * h, n)]

    def ring(ci, i):
        src, dev = {
            0: lambda: (rb(ci, z), ZP),
            1: lambda: (rb(ci, z), ZM),
            2: lambda: (rhalf(ci, zm, 0), ZP),
            3: lambda: (rhalf(ci, zp, 1), ZM),
        }[i]()
        return rcopy(src, src, zs.at[ci, i], zr.at[ci, i], dev)

    def ring_got(ci, i):
        dst = {
            0: lambda: rb(ci, zm),
            1: lambda: rb(ci, zp),
            2: lambda: rhalf(ci, (z + 2) % 4, 0),
            3: lambda: rhalf(ci, (z + 2) % 4, 1),
        }[i]()
        got(dst, zs.at[ci, i], zr.at[ci, i])

    def ring_a(ci):
        ring(ci, 0).start()
        ring(ci, 1).start()

    def ring_b(ci):
        ring_got(ci, 0)
        ring(ci, 2).start()
        ring_got(ci, 1)
        ring(ci, 3).start()

    def ring_c(ci):
        ring_got(ci, 2)
        ring_got(ci, 3)

    def own(dy, dz):
        return ((yh + dy) % 2) * 4 + (z + dz) % 4

    def ob(h, dy, dz):
        return wob.at[h, own(dy, dz)]

    def oh(h, dy, dz, k):
        return wob.at[h, own(dy, dz), pl.ds(1024 * k, 1024)]

    def osend(h, i):
        src, dev = {
            0: lambda: (ob(h, 0, 0), YP),
            1: lambda: (ob(h, 0, 0), ZP),
            2: lambda: (ob(h, 0, 0), ZM),
            3: lambda: (ob(h, 1, 0), ZP),
            4: lambda: (ob(h, 1, 0), ZM),
            5: lambda: (oh(h, 0, 3, 0), ZP),
            6: lambda: (oh(h, 0, 1, 1), ZM),
            7: lambda: (ob(h, 0, 2), YP),
        }[i]()
        return rcopy(src, src, os_.at[h, i], or_.at[h, i], dev)

    def ogot(h, i):
        dst = {
            0: lambda: ob(h, 1, 0),
            1: lambda: ob(h, 0, 3),
            2: lambda: ob(h, 0, 1),
            3: lambda: ob(h, 1, 3),
            4: lambda: ob(h, 1, 1),
            5: lambda: oh(h, 0, 2, 0),
            6: lambda: oh(h, 0, 2, 1),
            7: lambda: ob(h, 1, 2),
        }[i]()
        got(dst, os_.at[h, i], or_.at[h, i])

    def o_fill(h):
        return pltpu.make_async_copy(wo.at[:, pl.ds(128 * h, 128)], wob.at[h, b], ol.at[h])

    def o_az(h):
        o_fill(h).wait()
        osend(h, 1).start()
        osend(h, 2).start()

    def o_ay(h):
        osend(h, 0).start()

    def o_b1(h):
        ogot(h, 1)
        osend(h, 5).start()
        ogot(h, 2)
        osend(h, 6).start()

    def o_b2(h):
        ogot(h, 0)
        osend(h, 3).start()
        osend(h, 4).start()

    def o_zz(h):
        ogot(h, 5)
        ogot(h, 6)
        osend(h, 7).start()

    def o_c(h):
        ogot(h, 3)
        ogot(h, 4)

    def o_d(h):
        ogot(h, 7)

    for ci in (KV, QA, QB):
        for n in range(3):
            fill(ci, n).start()
        fill_local(ci).start()
    for h in (0, 1):
        o_fill(h).start()

    def segs(n):
        return rcopy(sgr.at[u], sgr.at[u], gs.at[n], gr.at[u], [YP, YX, SIB][n])

    sgr[u] = seg[...]
    for n in range(3):
        segs(n).start()

    def hid_cols(o, cc):
        return hid.at[:, pl.ds(al(256 * (2 * o + cc), 256), 256)]

    def hid_remote(o):
        return rcopy(hid_cols(o, oc), hf.at[c, o], hs.at[o], hr.at[o], SIB)

    def hid_local(o):
        return pltpu.make_async_copy(hid_cols(o, c), hf.at[c, o], hl.at[o])

    def norm(i, carry):
        r = pl.ds(al(32 * i, 32), 32)
        v = hid[r, :].astype(F32)
        v = v * lax.rsqrt(jnp.mean(v * v, axis=-1, keepdims=True) + 1e-05)
        v = v.astype(BF)
        dst = pl.ds(al(256 * u + 32 * i, 32), 32)
        for d in range(16):
            lanes = 256 * (2 * (d // 8) + d % 2)
            x[(d // 2) % 4, dst, lanes:lanes + 256] = v[:, 256 * d:256 * d + 256]
        return carry

    lax.fori_loop(0, 8, norm, 0)

    def xcopy(k, q):
        v, dev = [(u, YP), (u, SIB), (u_y, SIB)][k]
        ref = x.at[q, r256(v)]
        return rcopy(ref, ref, xs.at[k, q], xr.at[k, q], dev)

    def xgot(k, q):
        v = [u_y, u_sib, u_yx][k]
        got(x.at[q, r256(v)], xs.at[k, q], xr.at[k, q])

    for q in range(4):
        xcopy(0, q).start()
        xcopy(1, q).start()

    def x_forward(q):
        xgot(0, q)
        xcopy(2, q).start()

    acck[...] = jnp.zeros_like(acck)
    accq[...] = jnp.zeros_like(accq)

    def gemm(yr, lo, hi):
        rows = pl.ds(al(512 * yr, 512), 512)

        def step(q, carry):
            xv = x[q, rows, :]
            acck[rows, :] += jnp.dot(xv, wkvb[q], preferred_element_type=F32)
            for k in (0, 1):
                accq[k, rows, :] += jnp.dot(xv, wqb[k, q], preferred_element_type=F32)
            return carry

        lax.fori_loop(lo, hi, step, 0)

    for ci in (KV, QA, QB):
        fill_wait(ci)
        ring_a(ci)
    for o in range(8):
        hid_remote(o).start()
        hid_local(o).start()
    ring_b(KV)
    x_forward(0)
    ring_b(QA)
    for q in range(4):
        xgot(1, q)
    x_forward(1)
    ring_b(QB)
    o_az(0)
    ring_c(KV)
    ring_c(QA)
    x_forward(2)
    ring_c(QB)
    o_az(1)
    gemm(yh, 0, 4)
    xgot(2, 0)
    xgot(2, 1)
    gemm(oy, 0, 2)
    xgot(2, 2)
    gemm(oy, 2, 3)
    x_forward(3)
    o_ay(0)
    o_ay(1)
    xgot(2, 3)
    gemm(oy, 3, 4)
    kvb[z, 0:1024, :] = acck[...].astype(BF)
    for v in (u_sib, u_y, u_yx):
        got(sgr.at[v], gs.at[0], gr.at[v])
    for k in range(4):
        kvb[z, 1024 + 32 * k:1056 + 32 * k, :] = sgr[k]
    ring_a(KX)
    for p in range(4):
        qs[p] = accq[p // 2, :, 128 * (p % 2):128 * (p % 2) + 128].astype(BF)
    o_b1(0)
    ring_b(KX)
    o_b1(1)
    ring_c(KX)
    o_b2(0)

    lane = lax.broadcasted_iota(jnp.int32, (256, 128), 1)
    row = lax.broadcasted_iota(jnp.int32, (256, 128), 0)
    low = lane < 64
    below1 = jnp.zeros((16, 128), F32)
    below2 = jnp.zeros((16, 128), F32)
    for q in range(4):
        for t in range(1024, 1152, 16):
            g = kvb[q, t:t + 16, :].astype(F32)
            below1 = below1 + jnp.where(g < 0.5, 1.0, 0.0)
            below2 = below2 + jnp.where(g < 1.5, 1.0, 0.0)
    n1 = jnp.sum(below1[0:8], axis=-1, keepdims=True)[0:1, :]
    n2 = jnp.sum(below2[0:8], axis=-1, keepdims=True)[0:1, :]
    for r in range(4):
        g = jnp.concatenate(
            [jnp.transpose(jnp.broadcast_to(sgr[r, 16 * k:16 * k + 16, :].astype(F32)[0:1, :], (128, 128)))
             for k in (0, 1)], axis=0)
        start = jnp.where(g < 0.5, 0.0, jnp.where(g < 1.5, n1, n2)).astype(jnp.int32)
        pos = 2048 * (r // 2) + 512 * z + 256 * (r % 2) + row
        lod[r] = jnp.maximum(start, pos - 2047) - lane

    def attend(yr, cr, mine):
        r = 2 * yr + cr
        rblk = 2 * (4 * yr + z) + cr

        def one(p, carry):
            q2 = qs[p, r256(r), :].astype(F32)
            zero = jnp.zeros_like(q2)
            d1 = lod[r]
            for hh in (0, 1):
                q1 = jnp.where(low, q2 if hh == 0 else pltpu.roll(q2, 64, 1), zero).astype(BF)
                ss = []
                m = jnp.full((256, 128), -1e30, F32)
                for t in range(9):
                    kb = (rblk + t + 8) % 16
                    kk = kvb[(kb // 2) % 4, r256(2 * (kb // 8) + kb % 2), :]
                    s = lax.dot_general(q1, kk, (((1,), (1,)), ((), ())),
                                        preferred_element_type=F32)
                    base = 256 * (rblk + t) - 2048
                    for v in (0, 1):
                        ok = d1 <= base + 128 * v
                        if t == 8:
                            ok = ok & (row - lane >= 128 * v)
                        su = jnp.where(ok, s[:, 128 * v:128 * v + 128], -1e30)
                        ss.append(su)
                        m = jnp.maximum(m, su)
                mm = jnp.max(m, axis=-1, keepdims=True)
                l = jnp.zeros((256, 128), F32)
                o_ = jnp.zeros((256, 128), F32)
                for t in range(9):
                    kb = (rblk + t + 8) % 16
                    kk = kvb[(kb // 2) % 4, r256(2 * (kb // 8) + kb % 2), :]
                    w0 = jnp.exp2((ss[2 * t] - mm) * EXP_SCALE)
                    w1 = jnp.exp2((ss[2 * t + 1] - mm) * EXP_SCALE)
                    l = l + w0 + w1
                    o_ = o_ + jnp.dot(jnp.concatenate([w0, w1], axis=1).astype(BF), kk,
                                      preferred_element_type=F32)
                ostat[hh] = o_ / jnp.sum(l, axis=-1, keepdims=True)
            res = jnp.where(low, pltpu.roll(ostat[0], 64, 1), ostat[1]).astype(BF)
            if mine:
                att[r256(cr), pl.ds(al(512 * u + 128 * p, 128), 128)] = res
            else:
                atx[cr, :, pl.ds(al(128 * p, 128), 128)] = res
            return carry

        lax.fori_loop(0, 4, one, 0, unroll=2)

    def ablk(cr, v):
        return att.at[r256(cr), pl.ds(al(512 * v, 512), 512)]

    def acopy(k, cr):
        src, dst, dev = [
            lambda: (atx.at[cr], ablk(cr, u), YP),
            lambda: (ablk(cr, u), ablk(cr, u), SIB),
            lambda: (ablk(cr, u_y), ablk(cr, u_y), SIB),
        ][k]()
        return rcopy(src, dst, axs.at[k, cr], axr.at[k, cr], dev)

    def agot(k, cr):
        got(ablk(cr, [u_y, u_sib, u_yx][k]), axs.at[k, cr], axr.at[k, cr])

    def out_cols(o, cc, h):
        return out.at[:, pl.ds(al(256 * (2 * o + cc) + 128 * h, 128), 128)]

    def pass_copy(h, o, cr):
        return rcopy(outb.at[h, o, cr], out_cols(o, c, h), ps.at[h, o, cr], pr.at[h, o, c], NX[cr])

    def project(cr, h, n, dy, dz):
        def step(i, carry):
            o = own(dy(i), dz(i))
            v = jnp.dot(att[r256(cr), :], wob[h, o], preferred_element_type=F32)
            r = v + hf[cr, o, :, 128 * h:128 * h + 128].astype(F32)
            outb[h, o, cr] = r.astype(BF)
            if cr == 1:
                pass_copy(h, o, cr).start()
            else:
                @pl.when(jnp.logical_not(wrap))
                def _():
                    pass_copy(h, o, cr).start()

                @pl.when(wrap)
                def _():
                    rcopy(outb.at[h, o, cr], rly.at[h, o], ps.at[h, o, cr], rr.at[h, o], MID).start()

            return carry

        lax.fori_loop(0, n, step, 0)

    def project_b(cr, h):
        project(cr, h, 4, lambda i: 0, lambda i: i)
        project(cr, h, 1, lambda i: 1, lambda i: 0)

    def project_c(cr, h):
        project(cr, h, 2, lambda i: 1, lambda i: 1 + 2 * i)

    def project_d(cr, h):
        project(cr, h, 1, lambda i: 1, lambda i: 2)

    def relay_copy(h, o):
        return rcopy(rly.at[h, o], out_cols(o, c, h), rs.at[h, o], pr.at[h, o, c], FAR[0])

    def relay(h, n, dy, dz):
        @pl.when(wrap)
        def _():
            def step(i, carry):
                o = own(dy(i), dz(i))
                got(rly.at[h, o], rs.at[h, o], rr.at[h, o])
                relay_copy(h, o).start()
                return carry

            lax.fori_loop(0, n, step, 0)

    def relay_b(h):
        relay(h, 4, lambda i: 0, lambda i: i)
        relay(h, 1, lambda i: 1, lambda i: 0)

    def relay_c(h):
        relay(h, 2, lambda i: 1, lambda i: 1 + 2 * i)

    def relay_d(h):
        relay(h, 1, lambda i: 1, lambda i: 2)

    attend(oy, 0, False)
    acopy(0, 0).start()
    o_zz(0)
    o_b2(1)
    attend(yh, 0, True)
    acopy(1, 0).start()
    agot(0, 0)
    acopy(2, 0).start()
    o_zz(1)
    for o in range(8):
        hid_local(o).wait()
        got(hf.at[oc, o], hs.at[o], hr.at[o])
    agot(1, 0)
    agot(2, 0)
    project_b(0, 0)
    attend(oy, 1, False)
    acopy(0, 1).start()
    o_c(0)
    project_c(0, 0)
    o_d(0)
    project_d(0, 0)
    project_b(0, 1)
    relay_b(0)
    attend(yh, 1, True)
    acopy(1, 1).start()
    agot(0, 1)
    acopy(2, 1).start()
    relay_c(0)
    relay_d(0)
    relay_b(1)
    agot(1, 1)
    agot(2, 1)
    project_b(1, 0)
    project_c(1, 0)
    project_d(1, 0)
    project_b(1, 1)
    o_c(1)
    project_c(0, 1)
    project_c(1, 1)
    o_d(1)
    project_d(0, 1)
    project_d(1, 1)
    relay_c(1)
    relay_d(1)

    for ci in range(4):
        for i in range(4):
            ring(ci, i).wait_send()
        if ci < KX:
            for n in range(3):
                fill(ci, n).wait_send()
    for h in (0, 1):
        for i in range(8):
            osend(h, i).wait_send()
    for n in range(3):
        segs(n).wait_send()
    for k in range(3):
        for q in range(4):
            xcopy(k, q).wait_send()
        for cr in (0, 1):
            acopy(k, cr).wait_send()
    for o in range(8):
        hid_remote(o).wait_send()
    for h in (0, 1):
        for o in range(8):
            for cc in (0, 1):
                pass_copy(h, o, cc).wait_send()
                got(out_cols(o, cc, h), ps.at[h, o, cc], pr.at[h, o, cc])

    @pl.when(wrap)
    def _():
        for h in (0, 1):
            for o in range(8):
                relay_copy(h, o).wait_send()


def body(section_input, segment_ids, query_weight, keyval_weight, out_weight):
    seg = segment_ids[0].astype(BF).reshape(2, 1, 128)
    seg = jnp.broadcast_to(seg, (2, 16, 128)).reshape(32, 128)
    wkv = keyval_weight[0].reshape(256, 2, 4, 64).transpose(0, 2, 1, 3).reshape(256, 512)
    vm = pl.BlockSpec(memory_space=pltpu.VMEM)
    hb = pl.BlockSpec(memory_space=pl.ANY)
    dma = pltpu.SemaphoreType.DMA
    res = pl.pallas_call(
        kernel,
        out_shape=jax.ShapeDtypeStruct((256, 4096), BF),
        in_specs=[vm, vm, hb, hb, hb],
        out_specs=hb,
        scratch_shapes=[
            pltpu.VMEM((4, 1024, 1024), BF),
            pltpu.VMEM((2, 4, 1024, 256), BF),
            pltpu.VMEM((4, 1024, 128), BF),
            pltpu.VMEM((2, 8, 2048, 128), BF),
            pltpu.VMEM((4, 1152, 128), BF),
            pltpu.VMEM((4, 1024, 128), BF),
            pltpu.VMEM((512, 2048), BF),
            pltpu.VMEM((2, 256, 512), BF),
            pltpu.VMEM((2, 8, 256, 256), BF),
            pltpu.VMEM((2, 8, 2, 256, 128), BF),
            pltpu.VMEM((2, 1024, 256), F32),
            pltpu.VMEM((1024, 128), F32),
            pltpu.VMEM((2, 256, 128), F32),
            pltpu.VMEM((4, 32, 128), BF),
            pltpu.VMEM((4, 256, 128), jnp.int32),
            dma((3, 3)), dma((3, 4)), dma((3,)),
            dma((4, 4)), dma((4, 4)),
            dma((2, 8)), dma((2, 8)), dma((2,)),
            dma((3, 4)), dma((3, 4)),
            dma((8,)), dma((8,)), dma((8,)),
            dma((3,)), dma((4,)),
            dma((3, 2)), dma((3, 2)),
            dma((2, 8, 2)), dma((2, 8, 2)),
            pltpu.VMEM((2, 8, 256, 128), BF),
            dma((2, 8)), dma((2, 8)),
        ],
        compiler_params=pltpu.CompilerParams(
            collective_id=0, has_side_effects=True, vmem_limit_bytes=58 << 20),
        name="layer",
    )(section_input[0], seg, query_weight[0], wkv, out_weight[0])
    return res[None]


def solution(mesh):
    fine = Mesh(mesh.devices.reshape(8, 2, 4, 2), ("section", "yh", "z", "core"))
    tok = ("yh", "z", "core")
    return jax.shard_map(
        body,
        mesh=fine,
        in_specs=(
            P("section", tok, None),
            P("section", tok),
            P("section", tok, None),
            P("section", tok, None),
            P("section", None, tok),
        ),
        out_specs=P("section", tok, None),
        check_vma=False,
    )
```

time: 523 us -> 199 us (0.38)
  waiting for transfers between devices: 238 us -> 0 us
  Pallas kernels: 0 us -> 191 us
  matrix products: 130 us -> 0 us
  other arithmetic: 74.8 us -> 0.7 us
  local copies, waits for them, and re-layouts: 37.9 us -> 5.67 us
  blocking collectives: 20.1 us -> 0 us
  between operations: 13.2 us -> 0.03 us
  loops' own time: 6.13 us -> 0 us
    pallas_call x0 -> x1, Pallas kernels: none -> 191 us  [body(): pl.pallas_call(kernel, out_shape=jax.ShapeDtypeStruct((256, 4096), BF), i...]
    all_gather x4 -> x0, waiting for transfers between devices: 188 us -> none  [the longest x1 82.8 us: body(): lax.all_gather(query_weight, 'fsdp', axis=1, tiled=True)[0]]
    dot_general x19 -> x0, matrix products: 130 us -> none  [the longest x8 57.2 us: one_block(): jnp.einsum('qhgd,khd->hgqk', query_rows, key_lines, preferred_element_typ...]
    reduce_sum x9 -> x0, other arithmetic: 69.6 us -> none  [the longest x8 67.5 us: one_block(): sum_new = sum_now * factor + jnp.sum(weights, axis=-1)]
    ppermute x1 -> x0, waiting for transfers between devices: 47.7 us -> none  [from_behind(): return lax.ppermute(value, axis, pairs)]
    all_gather x1 -> x0, blocking collectives: 20.1 us -> none  [body(): key_segs = lax.all_gather(segments, 'fsdp', axis=0, tiled=True)]
    while x24 -> x0, local copies, waits for them, and re-layouts: 19.3 us -> none
    dynamic_slice x32 -> x0, local copies, waits for them, and re-layouts: 15.7 us -> none  [body(): lax.scan(one_block, start_state, (key_tiles, seg_blocks, jnp.arange(total...]
  transfers between devices with their start and end apart: 5 -> 0, of which waited for: 4 -> 0; matrix products, arithmetic and copies ran while one was open for 41% -> 0% of each run, Pallas kernels for 0% -> 0%
where the time goes in v2:
time: 199 us; the launch traced here: 197 us
  Pallas kernels  191 us (96%)
  local copies, waits for them, and re-layouts  5.67 us (3%)
    pallas_call x1, Pallas kernels, body(): pl.pallas_call(kernel, out_shape=jax.ShapeDtypeStruct((256, 4096), BF), i...  191 us
    unnamed x2, local copies, waits for them, and re-layouts  4.21 us

profile of v2, /device:TPU:1, one launch (start us, length us, event | category | flops | bytes accessed | tf_op | source)
XLA Modules:
  0.0 197.5 jit_solution(11917918552845438319)
XLA Ops:
  0.0 0.7 convert_reduce_fusion
  0.7 0.6 broadcast_in_dim.8
  1.3 1.1 copy.7
  2.4 0.8 copy.9.wkv
  3.3 191.1 %layer.1 = bf16[256,4096]{1,0:T(8,128)(2,1)} custom-call(bf16[256,4096]{1,0:T(8,128)(2,1)} %bitcast.11, bf16[32,128]{1,0:T(8,128)(2,1)} %bitcast.16, bf16[256,2048]{1,0:T(8,128)(2,1)} %bitcast.12, bf16[256,512]{1,0:T(8,128)(2,1)} %copy.9.wkv, bf16[2048,256]{1,0:T(8,128)(2,1)} %bitcast.13), custom_call_target="tpu_custom_call" | custom-call | tf_op jit(solution)/shard_map/layer/pallas_call | solution.py:522
  194.3 3.1 %copy.11 = bf16[1,256,4096]{2,1,0:T(8,128)(2,1)} copy(bf16[1,256,4096]{2,1,0:T(8,128)(2,1)} %bitcast.10) | data formatting | bytes 4194304
  (1 shorter events, 0.0 us)

commit v3 on v2

--- a/solution.py
+++ b/solution.py
@@ -10,12 +10,12 @@
 MESH = pl.DeviceIdType.MESH
 EXP_SCALE = 0.125 * 1.4426950408889634
 
-KV, QA, QB, KX = range(4)
+KV, QA, QB, KA, KB = range(5)
 
 
 def kernel(hid, seg, wq, wkv, wo, out,
            x, wqb, wkvb, wob, kvb, qs, att, atx, hf, outb, accq, acck, ostat, sgr, lod,
-           fs, fr, fl, zs, zr, os_, or_, ol, xs, xr, hs, hr, hl, gs, gr, axs, axr, ps, pr, rly, rs, rr):
+           fs, fr, fl, zs, zr, os_, or_, ol, xs, xr, hs, hr, hl, gs, gr, axs, axr, ps, pr):
     sec, yh, z, c = (lax.axis_index(n) for n in ("section", "yh", "z", "core"))
     oc, oy = 1 - c, 1 - yh
     u = 2 * yh + c
@@ -30,10 +30,6 @@
     nxt, prv = (sec + 1) % 8, (sec + 7) % 8
     NX = [(nxt, yh, z, 0), (nxt, yh, z, 1)]
     PV = [(prv, yh, z, 0), (prv, yh, z, 1)]
-    wrap = sec % 4 == 3
-    MID = ((sec + 4) % 8, yh, z, c)
-    FAR = [((sec + 5) % 8, yh, z, k) for k in (0, 1)]
-    NEAR = [((sec + 3) % 8, yh, z, k) for k in (0, 1)]
 
     def rcopy(src, dst, send, recv, dev):
         return pltpu.make_async_remote_copy(
@@ -50,9 +46,9 @@
         return pl.ds(al(256 * k, 256), 256)
 
     bar = pltpu.get_barrier_semaphore()
-    for d in [SIB, YP, YX, ZP, ZM, MID] + NX + PV + FAR + NEAR:
+    for d in [SIB, YP, YX, ZP, ZM] + NX + PV:
         pl.semaphore_signal(bar, inc=1, device_id=d, device_id_type=MESH)
-    pl.semaphore_wait(bar, 14)
+    pl.semaphore_wait(bar, 9)
 
     def quarter(ci, v):
         if ci == KV:
@@ -62,8 +58,10 @@
     def rb(ci, zo):
         if ci == KV:
             return wkvb.at[zo]
-        if ci == KX:
-            return kvb.at[zo]
+        if ci == KA:
+            return kvb.at[zo, yh]
+        if ci == KB:
+            return kvb.at[zo, oy, pl.ds(0, 512)]
         return wqb.at[ci - QA, zo]
 
     def fill(ci, n):
@@ -79,7 +77,9 @@
             got(rb(ci, z).at[r256(v)], fs.at[ci, 0], fr.at[ci, v])
 
     def rhalf(ci, zo, h):
-        n = 576 if ci == KX else 512
+        if ci == KB:
+            return kvb.at[zo, oy, pl.ds(256 * h, 256)]
+        n = 320 if ci == KA else 512
         return rb(ci, zo).at[pl.ds(n * h, n)]
 
     def ring(ci, i):
@@ -132,7 +132,8 @@
             4: lambda: (ob(h, 1, 0), ZM),
             5: lambda: (oh(h, 0, 3, 0), ZP),
             6: lambda: (oh(h, 0, 1, 1), ZM),
-            7: lambda: (ob(h, 0, 2), YP),
+            7: lambda: (oh(h, 1, 3, 0), ZP),
+            8: lambda: (oh(h, 1, 1, 1), ZM),
         }[i]()
         return rcopy(src, src, os_.at[h, i], or_.at[h, i], dev)
 
@@ -145,7 +146,8 @@
             4: lambda: ob(h, 1, 1),
             5: lambda: oh(h, 0, 2, 0),
             6: lambda: oh(h, 0, 2, 1),
-            7: lambda: ob(h, 1, 2),
+            7: lambda: oh(h, 1, 2, 0),
+            8: lambda: oh(h, 1, 2, 1),
         }[i]()
         got(dst, os_.at[h, i], or_.at[h, i])
 
@@ -174,14 +176,16 @@
     def o_zz(h):
         ogot(h, 5)
         ogot(h, 6)
-        osend(h, 7).start()
 
     def o_c(h):
         ogot(h, 3)
+        osend(h, 7).start()
         ogot(h, 4)
+        osend(h, 8).start()
 
     def o_d(h):
         ogot(h, 7)
+        ogot(h, 8)
 
     for ci in (KV, QA, QB):
         for n in range(3):
@@ -257,6 +261,14 @@
     for o in range(8):
         hid_remote(o).start()
         hid_local(o).start()
+    def keyvals_out(yr):
+        kvb[z, yr, 0:512, :] = acck[pl.ds(al(512 * yr, 512), 512), :].astype(BF)
+
+    def queries_out(yr):
+        rows = pl.ds(al(512 * yr, 512), 512)
+        for p in range(4):
+            qs[p, rows, :] = accq[p // 2, rows, 128 * (p % 2):128 * (p % 2) + 128].astype(BF)
+
     ring_b(KV)
     x_forward(0)
     ring_b(QA)
@@ -267,33 +279,24 @@
     o_az(0)
     ring_c(KV)
     ring_c(QA)
+    ring_c(QB)
+    gemm(yh, 0, 4)
+    keyvals_out(yh)
+    for v in (u_sib, u_y, u_yx):
+        got(sgr.at[v], gs.at[0], gr.at[v])
+    for k in range(4):
+        kvb[z, yh, 512 + 32 * k:544 + 32 * k, :] = sgr[k]
+    ring_a(KA)
     x_forward(2)
-    ring_c(QB)
-    o_az(1)
-    gemm(yh, 0, 4)
+    ring_b(KA)
+    queries_out(yh)
     xgot(2, 0)
     xgot(2, 1)
     gemm(oy, 0, 2)
     xgot(2, 2)
     gemm(oy, 2, 3)
-    x_forward(3)
-    o_ay(0)
-    o_ay(1)
-    xgot(2, 3)
-    gemm(oy, 3, 4)
-    kvb[z, 0:1024, :] = acck[...].astype(BF)
-    for v in (u_sib, u_y, u_yx):
-        got(sgr.at[v], gs.at[0], gr.at[v])
-    for k in range(4):
-        kvb[z, 1024 + 32 * k:1056 + 32 * k, :] = sgr[k]
-    ring_a(KX)
-    for p in range(4):
-        qs[p] = accq[p // 2, :, 128 * (p % 2):128 * (p % 2) + 128].astype(BF)
+    ring_c(KA)
     o_b1(0)
-    ring_b(KX)
-    o_b1(1)
-    ring_c(KX)
-    o_b2(0)
 
     lane = lax.broadcasted_iota(jnp.int32, (256, 128), 1)
     row = lax.broadcasted_iota(jnp.int32, (256, 128), 0)
@@ -301,8 +304,8 @@
     below1 = jnp.zeros((16, 128), F32)
     below2 = jnp.zeros((16, 128), F32)
     for q in range(4):
-        for t in range(1024, 1152, 16):
-            g = kvb[q, t:t + 16, :].astype(F32)
+        for t in range(512, 640, 16):
+            g = kvb[q, yh, t:t + 16, :].astype(F32)
             below1 = below1 + jnp.where(g < 0.5, 1.0, 0.0)
             below2 = below2 + jnp.where(g < 1.5, 1.0, 0.0)
     n1 = jnp.sum(below1[0:8], axis=-1, keepdims=True)[0:1, :]
@@ -315,6 +318,17 @@
         pos = 2048 * (r // 2) + 512 * z + 256 * (r % 2) + row
         lod[r] = jnp.maximum(start, pos - 2047) - lane
 
+    x_forward(3)
+    o_ay(0)
+    xgot(2, 3)
+    gemm(oy, 3, 4)
+    keyvals_out(oy)
+    ring_a(KB)
+    queries_out(oy)
+    ring_b(KB)
+    o_az(1)
+    ring_c(KB)
+
     def attend(yr, cr, mine):
         r = 2 * yr + cr
         rblk = 2 * (4 * yr + z) + cr
@@ -329,7 +343,7 @@
                 m = jnp.full((256, 128), -1e30, F32)
                 for t in range(9):
                     kb = (rblk + t + 8) % 16
-                    kk = kvb[(kb // 2) % 4, r256(2 * (kb // 8) + kb % 2), :]
+                    kk = kvb[(kb // 2) % 4, kb // 8, r256(kb % 2), :]
                     s = lax.dot_general(q1, kk, (((1,), (1,)), ((), ())),
                                         preferred_element_type=F32)
                     base = 256 * (rblk + t) - 2048
@@ -345,7 +359,7 @@
                 o_ = jnp.zeros((256, 128), F32)
                 for t in range(9):
                     kb = (rblk + t + 8) % 16
-                    kk = kvb[(kb // 2) % 4, r256(2 * (kb // 8) + kb % 2), :]
+                    kk = kvb[(kb // 2) % 4, kb // 8, r256(kb % 2), :]
                     w0 = jnp.exp2((ss[2 * t] - mm) * EXP_SCALE)
                     w1 = jnp.exp2((ss[2 * t + 1] - mm) * EXP_SCALE)
                     l = l + w0 + w1
@@ -387,17 +401,7 @@
             v = jnp.dot(att[r256(cr), :], wob[h, o], preferred_element_type=F32)
             r = v + hf[cr, o, :, 128 * h:128 * h + 128].astype(F32)
             outb[h, o, cr] = r.astype(BF)
-            if cr == 1:
-                pass_copy(h, o, cr).start()
-            else:
-                @pl.when(jnp.logical_not(wrap))
-                def _():
-                    pass_copy(h, o, cr).start()
-
-                @pl.when(wrap)
-                def _():
-                    rcopy(outb.at[h, o, cr], rly.at[h, o], ps.at[h, o, cr], rr.at[h, o], MID).start()
-
+            pass_copy(h, o, cr).start()
             return carry
 
         lax.fori_loop(0, n, step, 0)
@@ -412,83 +416,56 @@
     def project_d(cr, h):
         project(cr, h, 1, lambda i: 1, lambda i: 2)
 
-    def relay_copy(h, o):
-        return rcopy(rly.at[h, o], out_cols(o, c, h), rs.at[h, o], pr.at[h, o, c], FAR[0])
-
-    def relay(h, n, dy, dz):
-        @pl.when(wrap)
-        def _():
-            def step(i, carry):
-                o = own(dy(i), dz(i))
-                got(rly.at[h, o], rs.at[h, o], rr.at[h, o])
-                relay_copy(h, o).start()
-                return carry
-
-            lax.fori_loop(0, n, step, 0)
-
-    def relay_b(h):
-        relay(h, 4, lambda i: 0, lambda i: i)
-        relay(h, 1, lambda i: 1, lambda i: 0)
-
-    def relay_c(h):
-        relay(h, 2, lambda i: 1, lambda i: 1 + 2 * i)
-
-    def relay_d(h):
-        relay(h, 1, lambda i: 1, lambda i: 2)
-
     attend(oy, 0, False)
     acopy(0, 0).start()
-    o_zz(0)
-    o_b2(1)
-    attend(yh, 0, True)
-    acopy(1, 0).start()
+    o_ay(1)
+    o_b2(0)
+    attend(oy, 1, False)
+    acopy(0, 1).start()
+    o_b1(1)
     agot(0, 0)
     acopy(2, 0).start()
-    o_zz(1)
     for o in range(8):
         hid_local(o).wait()
         got(hf.at[oc, o], hs.at[o], hr.at[o])
+    attend(yh, 0, True)
+    acopy(1, 0).start()
+    agot(0, 1)
+    acopy(2, 1).start()
+    o_b2(1)
+    o_c(0)
+    o_zz(0)
     agot(1, 0)
     agot(2, 0)
     project_b(0, 0)
-    attend(oy, 1, False)
-    acopy(0, 1).start()
-    o_c(0)
     project_c(0, 0)
-    o_d(0)
-    project_d(0, 0)
-    project_b(0, 1)
-    relay_b(0)
+    o_zz(1)
     attend(yh, 1, True)
     acopy(1, 1).start()
-    agot(0, 1)
-    acopy(2, 1).start()
-    relay_c(0)
-    relay_d(0)
-    relay_b(1)
+    project_b(0, 1)
     agot(1, 1)
     agot(2, 1)
     project_b(1, 0)
     project_c(1, 0)
-    project_d(1, 0)
+    o_c(1)
     project_b(1, 1)
-    o_c(1)
     project_c(0, 1)
     project_c(1, 1)
+    o_d(0)
+    project_d(0, 0)
+    project_d(1, 0)
     o_d(1)
     project_d(0, 1)
     project_d(1, 1)
-    relay_c(1)
-    relay_d(1)
-
-    for ci in range(4):
+
+    for ci in range(5):
         for i in range(4):
             ring(ci, i).wait_send()
-        if ci < KX:
+        if ci < KA:
             for n in range(3):
                 fill(ci, n).wait_send()
     for h in (0, 1):
-        for i in range(8):
+        for i in range(9):
             osend(h, i).wait_send()
     for n in range(3):
         segs(n).wait_send()
@@ -504,12 +481,6 @@
             for cc in (0, 1):
                 pass_copy(h, o, cc).wait_send()
                 got(out_cols(o, cc, h), ps.at[h, o, cc], pr.at[h, o, cc])
-
-    @pl.when(wrap)
-    def _():
-        for h in (0, 1):
-            for o in range(8):
-                relay_copy(h, o).wait_send()
 
 
 def body(section_input, segment_ids, query_weight, keyval_weight, out_weight):
@@ -529,7 +500,7 @@
             pltpu.VMEM((2, 4, 1024, 256), BF),
             pltpu.VMEM((4, 1024, 128), BF),
             pltpu.VMEM((2, 8, 2048, 128), BF),
-            pltpu.VMEM((4, 1152, 128), BF),
+            pltpu.VMEM((4, 2, 640, 128), BF),
             pltpu.VMEM((4, 1024, 128), BF),
             pltpu.VMEM((512, 2048), BF),
             pltpu.VMEM((2, 256, 512), BF),
@@ -541,15 +512,13 @@
             pltpu.VMEM((4, 32, 128), BF),
             pltpu.VMEM((4, 256, 128), jnp.int32),
             dma((3, 3)), dma((3, 4)), dma((3,)),
-            dma((4, 4)), dma((4, 4)),
-            dma((2, 8)), dma((2, 8)), dma((2,)),
+            dma((5, 4)), dma((5, 4)),
+            dma((2, 9)), dma((2, 9)), dma((2,)),
             dma((3, 4)), dma((3, 4)),
             dma((8,)), dma((8,)), dma((8,)),
             dma((3,)), dma((4,)),
             dma((3, 2)), dma((3, 2)),
             dma((2, 8, 2)), dma((2, 8, 2)),
-            pltpu.VMEM((2, 8, 256, 128), BF),
-            dma((2, 8)), dma((2, 8)),
         ],
         compiler_params=pltpu.CompilerParams(
             collective_id=0, has_side_effects=True, vmem_limit_bytes=58 << 20),

time: 199 us -> 180 us (0.905)
  Pallas kernels: 191 us -> 173 us
    pallas_call x1, Pallas kernels: 191 us -> 173 us  [body(): pl.pallas_call(kernel, out_shape=jax.ShapeDtypeStruct((256, 4096), BF), i...]
where the time goes in v3:
time: 180 us; the launch traced here: 179 us
  Pallas kernels  173 us (96%)
  local copies, waits for them, and re-layouts  5.67 us (3%)
    pallas_call x1, Pallas kernels, body(): pl.pallas_call(kernel, out_shape=jax.ShapeDtypeStruct((256, 4096), BF), i...  173 us
    unnamed x2, local copies, waits for them, and re-layouts  4.21 us

profile of v3, /device:TPU:1, one launch (start us, length us, event | category | flops | bytes accessed | tf_op | source)
XLA Modules:
  0.0 179.4 jit_solution(16909690548631819583)
XLA Ops:
  0.0 0.7 convert_reduce_fusion
  0.7 0.6 broadcast_in_dim.8
  1.3 1.1 copy.7
  2.4 0.8 copy.9.wkv
  3.3 173.0 %layer.1 = bf16[256,4096]{1,0:T(8,128)(2,1)} custom-call(bf16[256,4096]{1,0:T(8,128)(2,1)} %bitcast.11, bf16[32,128]{1,0:T(8,128)(2,1)} %bitcast.16, bf16[256,2048]{1,0:T(8,128)(2,1)} %bitcast.12, bf16[256,512]{1,0:T(8,128)(2,1)} %copy.9.wkv, bf16[2048,256]{1,0:T(8,128)(2,1)} %bitcast.13), custom_call_target="tpu_custom_call" | custom-call | tf_op jit(solution)/shard_map/layer/pallas_call | solution.py:493
  176.3 3.1 %copy.11 = bf16[1,256,4096]{2,1,0:T(8,128)(2,1)} copy(bf16[1,256,4096]{2,1,0:T(8,128)(2,1)} %bitcast.10) | data formatting | bytes 4194304
  (1 shorter events, 0.0 us)

commit v4 on v3

--- a/solution.py
+++ b/solution.py
@@ -14,7 +14,7 @@
 
 
 def kernel(hid, seg, wq, wkv, wo, out,
-           x, wqb, wkvb, wob, kvb, qs, att, atx, hf, outb, accq, acck, ostat, sgr, lod,
+           x, wqb, wkvb, wob, kvb, qs, att, atx, hf, outb, accq, acck, ostat, sgr, lod, wkr,
            fs, fr, fl, zs, zr, os_, or_, ol, xs, xr, hs, hr, hl, gs, gr, axs, axr, ps, pr):
     sec, yh, z, c = (lax.axis_index(n) for n in ("section", "yh", "z", "core"))
     oc, oy = 1 - c, 1 - yh
@@ -45,6 +45,19 @@
     def r256(k):
         return pl.ds(al(256 * k, 256), 256)
 
+    lane = lax.broadcasted_iota(jnp.int32, (256, 128), 1)
+    row = lax.broadcasted_iota(jnp.int32, (256, 128), 0)
+    low = lane < 64
+
+    for j in (0, 1):
+        kp = wkv[:, 128 * j:128 * j + 128].astype(F32)
+        vp = wkv[:, 256 + 128 * j:384 + 128 * j].astype(F32)
+        wkr[2 * j] = jnp.where(low, kp, pltpu.roll(vp, 64, 1)).astype(BF)
+        wkr[2 * j + 1] = jnp.where(low, pltpu.roll(kp, 64, 1), vp).astype(BF)
+    for k in (0, 1):
+        part = jnp.broadcast_to(seg[0:1, 128 * k:128 * k + 128].astype(F32), (16, 128))
+        sgr[u, 16 * k:16 * k + 16, :] = part.astype(BF)
+
     bar = pltpu.get_barrier_semaphore()
     for d in [SIB, YP, YX, ZP, ZM] + NX + PV:
         pl.semaphore_signal(bar, inc=1, device_id=d, device_id_type=MESH)
@@ -52,7 +65,7 @@
 
     def quarter(ci, v):
         if ci == KV:
-            return wkv.at[:, pl.ds(al(128 * v, 128), 128)]
+            return wkr.at[v]
         return wq.at[:, pl.ds(al(512 * v + 256 * (ci - QA), 256), 256)]
 
     def rb(ci, zo):
@@ -197,7 +210,6 @@
     def segs(n):
         return rcopy(sgr.at[u], sgr.at[u], gs.at[n], gr.at[u], [YP, YX, SIB][n])
 
-    sgr[u] = seg[...]
     for n in range(3):
         segs(n).start()
 
@@ -298,9 +310,6 @@
     ring_c(KA)
     o_b1(0)
 
-    lane = lax.broadcasted_iota(jnp.int32, (256, 128), 1)
-    row = lax.broadcasted_iota(jnp.int32, (256, 128), 0)
-    low = lane < 64
     below1 = jnp.zeros((16, 128), F32)
     below2 = jnp.zeros((16, 128), F32)
     for q in range(4):
@@ -407,8 +416,11 @@
         lax.fori_loop(0, n, step, 0)
 
     def project_b(cr, h):
-        project(cr, h, 4, lambda i: 0, lambda i: i)
+        project(cr, h, 3, lambda i: 0, lambda i: i + i // 2)
         project(cr, h, 1, lambda i: 1, lambda i: 0)
+
+    def project_z(cr, h):
+        project(cr, h, 1, lambda i: 0, lambda i: 2)
 
     def project_c(cr, h):
         project(cr, h, 2, lambda i: 1, lambda i: 1 + 2 * i)
@@ -432,28 +444,32 @@
     acopy(1, 0).start()
     agot(0, 1)
     acopy(2, 1).start()
-    o_b2(1)
-    o_c(0)
     o_zz(0)
     agot(1, 0)
     agot(2, 0)
     project_b(0, 0)
+    o_c(0)
+    o_b2(1)
+    project_z(0, 0)
     project_c(0, 0)
-    o_zz(1)
+    project_b(0, 1)
     attend(yh, 1, True)
     acopy(1, 1).start()
-    project_b(0, 1)
+    o_zz(1)
+    project_z(0, 1)
     agot(1, 1)
     agot(2, 1)
     project_b(1, 0)
+    project_z(1, 0)
     project_c(1, 0)
+    project_b(1, 1)
+    project_z(1, 1)
     o_c(1)
-    project_b(1, 1)
-    project_c(0, 1)
-    project_c(1, 1)
     o_d(0)
     project_d(0, 0)
     project_d(1, 0)
+    project_c(0, 1)
+    project_c(1, 1)
     o_d(1)
     project_d(0, 1)
     project_d(1, 1)
@@ -484,16 +500,13 @@
 
 
 def body(section_input, segment_ids, query_weight, keyval_weight, out_weight):
-    seg = segment_ids[0].astype(BF).reshape(2, 1, 128)
-    seg = jnp.broadcast_to(seg, (2, 16, 128)).reshape(32, 128)
-    wkv = keyval_weight[0].reshape(256, 2, 4, 64).transpose(0, 2, 1, 3).reshape(256, 512)
     vm = pl.BlockSpec(memory_space=pltpu.VMEM)
     hb = pl.BlockSpec(memory_space=pl.ANY)
     dma = pltpu.SemaphoreType.DMA
     res = pl.pallas_call(
         kernel,
         out_shape=jax.ShapeDtypeStruct((256, 4096), BF),
-        in_specs=[vm, vm, hb, hb, hb],
+        in_specs=[vm, vm, hb, vm, hb],
         out_specs=hb,
         scratch_shapes=[
             pltpu.VMEM((4, 1024, 1024), BF),
@@ -511,6 +524,7 @@
             pltpu.VMEM((2, 256, 128), F32),
             pltpu.VMEM((4, 32, 128), BF),
             pltpu.VMEM((4, 256, 128), jnp.int32),
+            pltpu.VMEM((4, 256, 128), BF),
             dma((3, 3)), dma((3, 4)), dma((3,)),
             dma((5, 4)), dma((5, 4)),
             dma((2, 9)), dma((2, 9)), dma((2,)),
@@ -523,7 +537,7 @@
         compiler_params=pltpu.CompilerParams(
             collective_id=0, has_side_effects=True, vmem_limit_bytes=58 << 20),
         name="layer",
-    )(section_input[0], seg, query_weight[0], wkv, out_weight[0])
+    )(section_input[0], segment_ids, query_weight[0], keyval_weight[0], out_weight[0])
     return res[None]
 
 

time: 180 us -> 175 us (0.972)
  local copies, waits for them, and re-layouts: 5.67 us -> 3.13 us
  Pallas kernels: 173 us -> 171 us
    unnamed x2 -> x1, local copies, waits for them, and re-layouts: 4.21 us -> 3.13 us
where the time goes in v4:
time: 175 us
  Pallas kernels  171 us (98%)
  local copies, waits for them, and re-layouts  3.13 us (2%)
    pallas_call x1, Pallas kernels, body(): pl.pallas_call(kernel, out_shape=jax.ShapeDtypeStruct((256, 4096), BF), i...  171 us

profile of v4, /device:TPU:1, one launch (start us, length us, event | category | flops | bytes accessed | tf_op | source)
XLA Modules:
  0.0 174.6 jit_solution(8606506554617050783)
XLA Ops:
  0.0 171.5 %layer.1 = bf16[256,4096]{1,0:T(8,128)(2,1)} custom-call(bf16[256,4096]{1,0:T(8,128)(2,1)} %bitcast.6, s32[1,256]{1,0:T(1,128)} %seg.1, bf16[256,2048]{1,0:T(8,128)(2,1)} %bitcast.7, bf16[256,512]{1,0:T(8,128)(2,1)} %bitcast.9, bf16[2048,256]{1,0:T(8,128)(2,1)} %bitcast.8), custom_call_target="tpu_custom_call" | custom-call | tf_op jit(solution)/shard_map/layer/pallas_call | solution.py:506
  171.5 3.1 %copy.7 = bf16[1,256,4096]{2,1,0:T(8,128)(2,1)} copy(bf16[1,256,4096]{2,1,0:T(8,128)(2,1)} %bitcast.5) | data formatting | bytes 4194304

commit v5 on v4

--- a/solution.py
+++ b/solution.py
@@ -330,9 +330,12 @@
     x_forward(3)
     o_ay(0)
     xgot(2, 3)
-    gemm(oy, 3, 4)
+    last = pl.ds(al(512 * oy, 512), 512)
+    acck[last, :] += jnp.dot(x[3, last, :], wkvb[3], preferred_element_type=F32)
     keyvals_out(oy)
     ring_a(KB)
+    for k in (0, 1):
+        accq[k, last, :] += jnp.dot(x[3, last, :], wqb[k, 3], preferred_element_type=F32)
     queries_out(oy)
     ring_b(KB)
     o_az(1)

time: 175 us -> 175 us (level)
  no operation moved by 1% of the time
where the time goes in v5:
time: 175 us
  Pallas kernels  171 us (98%)
  local copies, waits for them, and re-layouts  3.13 us (2%)
    pallas_call x1, Pallas kernels, body(): pl.pallas_call(kernel, out_shape=jax.ShapeDtypeStruct((256, 4096), BF), i...  171 us

profile of v5, /device:TPU:1, one launch (start us, length us, event | category | flops | bytes accessed | tf_op | source)
XLA Modules:
  0.0 174.6 jit_solution(10582991813606197488)
XLA Ops:
  0.0 171.5 %layer.1 = bf16[256,4096]{1,0:T(8,128)(2,1)} custom-call(bf16[256,4096]{1,0:T(8,128)(2,1)} %bitcast.6, s32[1,256]{1,0:T(1,128)} %seg.1, bf16[256,2048]{1,0:T(8,128)(2,1)} %bitcast.7, bf16[256,512]{1,0:T(8,128)(2,1)} %bitcast.9, bf16[2048,256]{1,0:T(8,128)(2,1)} %bitcast.8), custom_call_target="tpu_custom_call" | custom-call | tf_op jit(solution)/shard_map/layer/pallas_call | solution.py:509
  171.5 3.1 %copy.7 = bf16[1,256,4096]{2,1,0:T(8,128)(2,1)} copy(bf16[1,256,4096]{2,1,0:T(8,128)(2,1)} %bitcast.5) | data formatting | bytes 4194304
